TPU v7x, 32 devices: a whole 2x2x4 slice. The times are simulated.
32 devices in a mesh: row: 8 (over y, x, core), col: 4 (over z).
Axes of the slice: x: 2, y: 2, z: 4, core: 2. Of those that a mesh axis runs over, the one named last changes fastest.
Arguments:
- images: bfloat16 [16384, 768], P(('row', 'col')), may hold values from -2 to 2
- weight_in: bfloat16 [768, 2048], replicated, may hold values from -0.21875 to 0.21875
- bias_in: float32 [2048], replicated, may hold values from -3 to 3
- weight_out: bfloat16 [2048, 256], replicated, may hold values from -0.125 to 0.125
- feature_scale: float32 [256], replicated, may hold values from 0.05 to 0.25
- position: int32 [16384], P(('row', 'col')), may hold values from 0 to 16383, as said below
Outputs:
- panel_tiles: float32 [16, 1024, 2, 512], P(None, 'row', None, 'col')
- next_tiles: float32 [16, 1024, 2, 512], P(None, 'row', None, 'col')
Inputs may be any that keep to these rules, and one draw needn't show every extreme that they name: position is a permutation of the kernel rows. Among the images of one device (each aligned block of 512 images) exactly 64 have a position whose tile index, position // 128, leaves a given remainder modulo the number of devices along row, for every remainder.
All inputs are finite; a program needn't handle non-finite values.
Results may differ from a plain program's by a relative error of at most 0.0057.
Values may be sent and summed in bfloat16 or wider, within the bound.
No kernel may reach another device: no remote copies, remote signals or barrier semaphores. Data moves between devices by JAX's collectives and lax.ppermute only.
A program may use at most 128 MiB of HBM per device.

v0:
```python
import jax
import jax.numpy as jnp
from jax import lax
from jax.sharding import PartitionSpec as P

TILE = 128
PANEL = 1024


noise_var = 0.5


def kernel_block(left_feats, right_feats):
    left_norm = jnp.sum(jnp.square(left_feats.astype(jnp.float32)), axis=1)
    right_norm = jnp.sum(jnp.square(right_feats.astype(jnp.float32)), axis=1)
    cross_block = jnp.dot(left_feats, right_feats.T, preferred_element_type=jnp.float32)
    distance = left_norm[:, None] + right_norm[None, :] - 2.0 * cross_block
    return jnp.exp(-0.5 * jnp.maximum(distance, 0.0))


def per_device(images, weight_in, bias_in, weight_out, feature_scale, position):
    image_rows = images.shape[0]
    feat_width = weight_out.shape[1]
    row_count = lax.axis_size("row")
    col_count = lax.axis_size("col")
    row_index = lax.axis_index("row")
    col_index = lax.axis_index("col")
    preact = jnp.dot(images, weight_in, preferred_element_type=jnp.float32) + bias_in
    hidden = jax.nn.gelu(preact, approximate=True).astype(jnp.bfloat16)
    features = (
        jnp.dot(hidden, weight_out, preferred_element_type=jnp.float32) * feature_scale
    ).astype(jnp.bfloat16)
    row_share = image_rows // row_count
    tile_group = position // TILE % row_count
    ordering = jnp.argsort(tile_group, stable=True)
    bucket = features[ordering].reshape(row_count, row_share, feat_width)
    places = position[ordering].reshape(row_count, row_share)
    widened = jnp.broadcast_to(bucket[:, None], (row_count, col_count, row_share, feat_width))
    widened = widened.reshape(row_count * col_count, row_share, feat_width)
    widened_places = jnp.broadcast_to(places[:, None], (row_count, col_count, row_share))
    widened_places = widened_places.reshape(row_count * col_count, row_share)
    received, received_places = (
        lax.all_to_all(widened, ("row", "col"), split_axis=0, concat_axis=0, tiled=True),
        lax.all_to_all(widened_places, ("row", "col"), split_axis=0, concat_axis=0, tiled=True),
    )
    received = received.reshape(-1, feat_width)
    received_places = received_places.reshape(-1)
    local_rows = image_rows * col_count
    slot_index = received_places // TILE // row_count * TILE + received_places % TILE
    owned = jnp.zeros((local_rows, feat_width), jnp.bfloat16).at[slot_index].set(received)
    lead_tiles = 2 * PANEL // (TILE * row_count)
    leading = owned[: lead_tiles * TILE].reshape(lead_tiles, TILE, feat_width)
    columns = lax.all_gather(leading, "row", axis=1, tiled=True).reshape(2 * PANEL, feat_width)
    row_iota = jnp.arange(local_rows, dtype=jnp.int32)
    local_place = (row_iota // TILE * row_count + row_index) * TILE + row_iota % TILE
    panel_iota = jnp.arange(PANEL, dtype=jnp.int32)
    kern_panel = kernel_block(owned, columns[:PANEL])
    kern_panel = kern_panel + jnp.where(local_place[:, None] == panel_iota[None, :], noise_var, 0.0)
    block_diag = kernel_block(columns[:PANEL], columns[:PANEL]) + noise_var * jnp.eye(
        PANEL, dtype=jnp.float32
    )
    factor = jnp.linalg.cholesky(block_diag)
    width_own = PANEL // col_count
    col_tiles = width_own // TILE
    own_index = jnp.arange(width_own, dtype=jnp.int32)
    own_columns = own_index // TILE * col_count * TILE + col_index * TILE + own_index % TILE
    picker = (panel_iota[:, None] == own_columns[None, :]).astype(jnp.float32)
    inverse_cols = jax.scipy.linalg.solve_triangular(factor, picker, lower=True, trans=1)
    panel_own = jnp.dot(kern_panel, inverse_cols, precision=lax.Precision.HIGHEST)
    next_feats = columns[PANEL:].reshape(col_tiles, col_count, TILE, feat_width)
    next_feats = lax.dynamic_index_in_dim(next_feats, col_index, 1, keepdims=False).reshape(
        width_own, feat_width
    )
    kern_next = kernel_block(owned, next_feats)
    kern_next = kern_next + jnp.where(
        local_place[:, None] == (PANEL + own_columns)[None, :], noise_var, 0.0
    )
    cross_block = kernel_block(columns[:PANEL], next_feats)
    solved = jax.scipy.linalg.cho_solve((factor, True), cross_block)
    update_own = kern_next - jnp.dot(kern_panel, solved, precision=lax.Precision.HIGHEST)
    local_tiles = local_rows // TILE
    shape_out = (local_tiles, TILE, col_tiles, TILE)
    return (panel_own.reshape(shape_out), update_own.reshape(shape_out))


def solution(mesh):
    in_specs = (P(("row", "col"), None), P(), P(), P(), P(), P(("row", "col")))
    out_specs = (P(None, "row", None, "col"), P(None, "row", None, "col"))
    return jax.shard_map(
        per_device, mesh=mesh, in_specs=in_specs, out_specs=out_specs, check_vma=False
    )
```

profile of v0, /device:TPU:11, one launch (start us, length us, event | category | flops | bytes accessed | tf_op | source)
XLA Modules:
  0.0 509.1 jit_solution(12667725823785193582)
XLA Ops:
  8.0 3.8 sort.17
  11.8 3.6 gather_fusion
  16.1 6.3 %all-to-all-start = ((s32[32,1,64]{2,1,0:T(1,128)}), s32[32,1,64]{2,1,0:T(1,128)S(1)}, u32[]{:S(2)}, u32[]{:S(2)}) async-start(s32[32,1,64]{2,1,0:T(1,128)} %bitcast), calls=%async_computation | async-start | bytes 32768 | tf_op jit(solution)/shard_map/all_to_all | solution.py:44
  22.5 4.1 fusion.18
  29.7 5.8 %all-to-all-start.1 = ((bf16[32,64,256]{2,1,0:T(8,128)(2,1)}), bf16[32,64,256]{2,1,0:T(8,128)(2,1)S(1)}, u32[]{:S(2)}, u32[]{:S(2)}) async-start(bf16[32,64,256]{2,1,0:T(8,128)(2,1)} %bitcast.3), calls=%async_computation.1 | async-start | bytes 2097152 | tf_op jit(solution)/shard_map/all_to_all | solution.py:43
  37.0 23.3 %all-to-all-done.1 = bf16[32,64,256]{2,1,0:T(8,128)(2,1)S(1)} async-done(((bf16[32,64,256]{2,1,0:T(8,128)(2,1)}), bf16[32,64,256]{2,1,0:T(8,128)(2,1)S(1)}, u32[]{:S(2)}, u32[]{:S(2)}) %all-to-all-start.1) | async-done | bytes 1048608 | tf_op jit(solution)/shard_map/all_to_all | solution.py:43
  60.2 9.8 %scatter_custom_fusion = bf16[2048,256]{1,0:T(8,128)(2,1)S(1)} fusion(s32[2048]{0:T(1024)S(1)} %bitcast.209, bf16[2048,256]{1,0:T(8,128)(2,1)S(1)} %bitcast.204, bf16[]{:T(256)} %constant.400.clone.1), kind=kCustom, calls=%fused_computation.104 | custom fusion | bytes 1048578 | tf_op jit(solution)/shard_map/scatter | solution.py:50
  72.3 22.2 %all-gather.2.cloned.1.call-done = bf16[2,1024,256]{2,1,0:T(8,128)(2,1)} async-done(((bf16[2,128,256]{2,1,0:T(8,128)(2,1)}), bf16[2,1024,256]{2,1,0:T(8,128)(2,1)}) %all-gather.2.cloned.1.call-update) | async-done | bytes 1048592 | tf_op jit(solution)/shard_map/all_gather | solution.py:53
  95.7 6.6 %broadcast_add_fusion = (f32[1024,1024]{0,1:T(8,128)}, f32[1024,1024]{0,1:T(8,128)}, f32[1024,1024]{1,0:T(8,128)}) fusion(f32[1024]{0:T(1024)S(1)} %multiply_reduce_fusion.1, bf16[2,1024,256]{2,1,0:T(8,128)(2,1)} %all-gather.2.cloned.1.call-done), kind=kOutput, calls=%fused_computation.29 | convolution fusion | flops 540016640 | bytes 13115392 | tf_op jit(solution)/shard_map/dot_general | solution.py:16
  102.3 5.3 %copy.14 = f32[1024,1024]{1,0:T(8,128)} copy(f32[1024,1024]{0,1:T(8,128)} %get-tuple-element.80) | data formatting | bytes 8388608 | tf_op jit(solution)/shard_map/add | solution.py:17
  107.6 5.4 %copy.15 = f32[1024,1024]{1,0:T(8,128)} copy(f32[1024,1024]{0,1:T(8,128)} %get-tuple-element.81) | data formatting | bytes 8388608 | tf_op jit(solution)/shard_map/sub | solution.py:17
  113.0 5.9 %add_multiply_fusion = f32[1024,1024]{1,0:T(8,128)S(1)} fusion(f32[1024,1024]{1,0:T(8,128)} %copy.15, f32[1024,1024]{1,0:T(8,128)} %copy.14, f32[1024,1024]{1,0:T(8,128)} %get-tuple-element.82), kind=kLoop, calls=%fused_computation.19 | loop fusion | flops 14680064 | bytes 16777216 | tf_op jit(solution)/shard_map/jit(cholesky)/div | solution.py:62
  120.9 11.7 %cholesky.222 = f32[128,128]{1,0:T(8,128)S(1)} custom-call(f32[128,128]{1,0:T(8,128)S(1)} %cholesky.577), custom_call_target="Cholesky" | custom-call | tf_op jit(solution)/shard_map/jit(cholesky)/cholesky | solution.py:62
  132.6 9.8 %custom-call.66 = f32[1,128,128]{1,2,0:T(8,128)S(1)} custom-call(f32[1,128,128]{2,1,0:T(8,128)S(1)} %get-tuple-element.79), custom_call_target="InvertDiagBlocksLowerTriangular" | custom-call | tf_op jit(solution)/shard_map/jit(cholesky)/cholesky | solution.py:62
  142.5 2.5 cholesky.254
  145.0 2.4 constant_dynamic-update-slice_fusion.74
  148.9 11.7 %cholesky.243 = f32[128,128]{1,0:T(8,128)S(1)} custom-call(f32[128,128]{1,0:T(8,128)S(1)} %cholesky.581), custom_call_target="Cholesky" | custom-call | tf_op jit(solution)/shard_map/jit(cholesky)/cholesky | solution.py:62
  161.3 18.5 %custom-call.67 = f32[1,128,128]{1,2,0:T(8,128)S(1)} custom-call(f32[1,128,128]{2,1,0:T(8,128)S(1)} %get-tuple-element.76), custom_call_target="InvertDiagBlocksLowerTriangular" | custom-call | tf_op jit(solution)/shard_map/jit(cholesky)/cholesky | solution.py:62
  183.1 11.7 %cholesky.466 = f32[128,128]{1,0:T(8,128)S(1)} custom-call(f32[128,128]{1,0:T(8,128)S(1)} %cholesky.586), custom_call_target="Cholesky" | custom-call | tf_op jit(solution)/shard_map/jit(cholesky)/cholesky | solution.py:62
  196.1 9.8 %custom-call.68 = f32[1,128,128]{1,2,0:T(8,128)S(1)} custom-call(f32[1,128,128]{2,1,0:T(8,128)S(1)} %get-tuple-element.73), custom_call_target="InvertDiagBlocksLowerTriangular" | custom-call | tf_op jit(solution)/shard_map/jit(cholesky)/cholesky | solution.py:62
  207.1 2.3 convolution_subtract_fusion.2
  209.4 11.9 %cholesky.485 = f32[128,128]{1,0:T(8,128)S(1)} custom-call(f32[128,128]{1,0:T(8,128)S(1)} %cholesky.591), custom_call_target="Cholesky" | custom-call | tf_op jit(solution)/shard_map/jit(cholesky)/cholesky | solution.py:62
  222.6 9.8 %custom-call.69 = f32[1,128,128]{1,2,0:T(8,128)S(1)} custom-call(f32[1,128,128]{2,1,0:T(8,128)S(1)} %get-tuple-element.70), custom_call_target="InvertDiagBlocksLowerTriangular" | custom-call | tf_op jit(solution)/shard_map/jit(cholesky)/cholesky | solution.py:62
  235.9 11.7 %cholesky.504 = f32[128,128]{1,0:T(8,128)S(1)} custom-call(f32[128,128]{1,0:T(8,128)S(1)} %cholesky.596), custom_call_target="Cholesky" | custom-call | tf_op jit(solution)/shard_map/jit(cholesky)/cholesky | solution.py:62
  248.9 9.8 %custom-call.70 = f32[1,128,128]{1,2,0:T(8,128)S(1)} custom-call(f32[1,128,128]{2,1,0:T(8,128)S(1)} %get-tuple-element.67), custom_call_target="InvertDiagBlocksLowerTriangular" | custom-call | tf_op jit(solution)/shard_map/jit(cholesky)/cholesky | solution.py:62
  259.7 2.7 convolution_subtract_fusion.4
  262.5 11.7 %cholesky.524 = f32[128,128]{1,0:T(8,128)S(1)} custom-call(f32[128,128]{1,0:T(8,128)S(1)} %cholesky.601), custom_call_target="Cholesky" | custom-call | tf_op jit(solution)/shard_map/jit(cholesky)/cholesky | solution.py:62
  275.5 9.8 %custom-call.71 = f32[1,128,128]{1,2,0:T(8,128)S(1)} custom-call(f32[1,128,128]{2,1,0:T(8,128)S(1)} %get-tuple-element.64), custom_call_target="InvertDiagBlocksLowerTriangular" | custom-call | tf_op jit(solution)/shard_map/jit(cholesky)/cholesky | solution.py:62
  288.3 11.7 %cholesky.544 = f32[128,128]{1,0:T(8,128)S(1)} custom-call(f32[128,128]{1,0:T(8,128)S(1)} %cholesky.606), custom_call_target="Cholesky" | custom-call | tf_op jit(solution)/shard_map/jit(cholesky)/cholesky | solution.py:62
  301.2 10.0 %custom-call.72 = f32[1,128,128]{1,2,0:T(8,128)S(1)} custom-call(f32[1,128,128]{2,1,0:T(8,128)S(1)} %get-tuple-element.61), custom_call_target="InvertDiagBlocksLowerTriangular" | custom-call | tf_op jit(solution)/shard_map/jit(cholesky)/cholesky | solution.py:62
  313.8 11.7 %cholesky.562 = f32[128,128]{1,0:T(8,128)S(1)} custom-call(f32[128,128]{1,0:T(8,128)S(1)} %convolution_subtract_fusion.27), custom_call_target="Cholesky" | custom-call | tf_op jit(solution)/shard_map/jit(cholesky)/cholesky | solution.py:62
  332.4 4.9 select_select_fusion
  337.3 27.9 %while.5 = (s32[]{:T(128)}, f32[1024,1024]{1,0:T(8,128)}, s32[8,2]{0,1:T(2,128)S(1)}, f32[8,128,128]{2,1,0:T(8,128)}, s32[]{:T(128)}) while((s32[]{:T(128)}, f32[1024,1024]{1,0:T(8,128)}, s32[8,2]{0,1:T(2,128)S(1)}, f32[8,128,128]{2,1,0:T(8,128)}, s32[]{:T(128)}) %tuple.74), condition=%wide.while_cond, body=%wide.while_body.sunk | while | flops 2 | bytes 132705 | solution.py:68
  337.9 2.9 bitcast_dynamic-update-slice_fusion.2
  341.4 2.9 bitcast_dynamic-update-slice_fusion.2
  344.9 2.9 bitcast_dynamic-update-slice_fusion.2
  348.4 2.9 bitcast_dynamic-update-slice_fusion.2
  351.9 2.9 bitcast_dynamic-update-slice_fusion.2
  355.4 2.9 bitcast_dynamic-update-slice_fusion.2
  358.9 2.9 bitcast_dynamic-update-slice_fusion.2
  362.4 2.8 bitcast_dynamic-update-slice_fusion.2
  365.2 79.6 %custom-call.75 = f32[8,128,128]{1,2,0:T(8,128)S(1)} custom-call(f32[8,128,128]{2,1,0:T(8,128)} %get-tuple-element.27), custom_call_target="InvertDiagBlocksLowerTriangular" | custom-call | tf_op jit(solution)/shard_map/jit(_solve_triangular)/triangular_solve/custom-call.1 | solution.py:68
  459.7 3.6 select_add_fusion
  463.3 6.9 %fusion.175 = f32[2048,256]{1,0:T(8,128)S(1)} fusion(f32[2048,1024]{1,0:T(8,128)S(1)} %select_add_fusion, f32[1024,256]{1,0:T(8,128)S(1)} %constant_dynamic-update-slice_fusion.61), kind=kOutput, calls=%fused_computation.375 | convolution fusion | flops 6442450944 | bytes 11534336 | tf_op jit(solution)/shard_map/dot_general | solution.py:80
  470.3 2.8 fusion.13
  473.1 3.5 reshape.361
  490.5 8.3 %fusion.174 = f32[2048,256]{1,0:T(8,128)} fusion(f32[2048,1024]{1,0:T(8,128)S(1)} %bitcast.202, f32[1024,256]{1,0:T(8,128)S(1)} %constant_dynamic-update-slice_fusion.18), kind=kOutput, calls=%fused_computation.374 | convolution fusion | flops 6442450944 | bytes 11534336 | tf_op jit(solution)/shard_map/dot_general | solution.py:69
  498.8 3.2 reshape.358
  (190 shorter events, 69.5 us)
Async XLA Ops:
  7.2 15.3 %copy-start = (bf16[768,2048]{1,0:T(8,128)(2,1)S(1)}, bf16[768,2048]{1,0:T(8,128)(2,1)}, u32[]{:S(2)}) copy-start(bf16[768,2048]{1,0:T(8,128)(2,1)} %param.9) | copy-start | bytes 9437188
  16.1 12.5 %all-to-all-start = ((s32[32,1,64]{2,1,0:T(1,128)}), s32[32,1,64]{2,1,0:T(1,128)S(1)}, u32[]{:S(2)}, u32[]{:S(2)}) async-start(s32[32,1,64]{2,1,0:T(1,128)} %bitcast), calls=%async_computation | async-start | bytes 32768 | tf_op jit(solution)/shard_map/all_to_all | solution.py:44
  29.7 30.5 %all-to-all-start.1 = ((bf16[32,64,256]{2,1,0:T(8,128)(2,1)}), bf16[32,64,256]{2,1,0:T(8,128)(2,1)S(1)}, u32[]{:S(2)}, u32[]{:S(2)}) async-start(bf16[32,64,256]{2,1,0:T(8,128)(2,1)} %bitcast.3), calls=%async_computation.1 | async-start | bytes 2097152 | tf_op jit(solution)/shard_map/all_to_all | solution.py:43
  35.5 58.9 %all-gather.2.cloned.1.call-start = ((), (), s32[]{:S(2)}) async-start(), calls=%async_computation.2 | async-start | bytes 1179648 | tf_op jit(solution)/shard_map/all_gather | solution.py:53
  119.0 1.9 copy-start.4
  332.3 112.5 %slice-start.2 = ((bf16[2,1024,256]{2,1,0:T(8,128)(2,1)}), bf16[1,1024,256]{2,1,0:T(8,128)(2,1)S(1)}, s32[]{:S(2)}) async-start(bf16[2,1024,256]{2,1,0:T(8,128)(2,1)} %all-gather.2.cloned.1.call-done), calls=%async_computation.5 | async-start | bytes 1048576 | tf_op jit(solution)/shard_map/slice | solution.py:70
  444.8 14.5 %copy-start.5 = (f32[8,128,128]{1,2,0:T(8,128)}, f32[8,128,128]{1,2,0:T(8,128)S(1)}, u32[]{:S(2)}) copy-start(f32[8,128,128]{1,2,0:T(8,128)S(1)} %custom-call.75) | copy-start | bytes 1572868
  444.8 2.5 copy-start.3
  457.0 2.7 copy-start.8
  463.3 6.9 %copy-start.2 = (f32[2048,1024]{1,0:T(8,128)}, f32[2048,1024]{1,0:T(8,128)S(1)}, u32[]{:S(2)}) copy-start(f32[2048,1024]{1,0:T(8,128)S(1)} %select_add_fusion) | copy-start | bytes 25165828
  473.1 3.5 copy-start.6
  473.1 3.5 copy-start.7
  478.1 12.4 %slice-start = ((s8[8388608]{0:T(1024)(128)(4,1)}), s8[4194304]{0:T(1024)(128)(4,1)S(1)}, s32[]{:S(2)}) async-start(s8[8388608]{0:T(1024)(128)(4,1)} %bitcast.201), calls=%async_computation.3 | async-start | bytes 8388608
  485.7 4.8 slice-start.1
  490.5 11.5 %copy-start.1 = (bf16[768,2048]{1,0:T(8,128)(2,1)S(1)}, bf16[768,2048]{1,0:T(8,128)(2,1)}, u32[]{:S(2)}) copy-start(bf16[768,2048]{1,0:T(8,128)(2,1)} %param.9) | copy-start | bytes 9437188
Sparse Core Ops, SparseCore 0:
  70.9 23.5 all-gather.1
where the time goes:
time: 519 us; the launch traced here: 509 us
  other arithmetic  279 us (54%)
  matrix products  82.9 us (16%)
  local copies, waits for them, and re-layouts  69.2 us (13%)
  waiting for transfers between devices  45.5 us (9%)
  between operations  20.2 us (4%)
  starting transfers between devices  12.2 us (2%)
    another operation x30, other arithmetic, per_device(): factor = jnp.linalg.cholesky(block_diag)  180 us
    another operation x4, other arithmetic, per_device(): jax.scipy.linalg.solve_triangular(factor, picker, lower=True, trans=1)  84.5 us
    another operation x29, local copies, waits for them, and re-layouts, per_device(): jax.scipy.linalg.solve_triangular(factor, picker, lower=True, trans=1)  28 us
    another operation x14, matrix products, per_device(): factor = jnp.linalg.cholesky(block_diag)  23.5 us
    all_to_all x1, waiting for transfers between devices, per_device(): lax.all_to_all(widened, ('row', 'col'), split_axis=0, concat_axis=0, tile...  23.3 us
    all_gather x1, waiting for transfers between devices, per_device(): lax.all_gather(leading, 'row', axis=1, tiled=True)  22.2 us
    dot_general x4, matrix products, kernel_block(): jnp.dot(left_feats, right_feats.T, preferred_element_type=jnp.float32)  14.8 us
    another operation x15, matrix products, per_device(): jax.scipy.linalg.solve_triangular(factor, picker, lower=True, trans=1)  13.3 us
  transfers between devices with their start and end apart: 3, of which 2 were waited for; matrix products, arithmetic and copies ran while one was open for 2% of the time, Pallas kernels for 0%

commit v1 on v0

v1 whole, which is shorter than its diff:
```python
import functools

import jax
import jax.numpy as jnp
from jax import lax
from jax.experimental import pallas as pl
from jax.experimental.pallas import tpu as pltpu
from jax.sharding import PartitionSpec as P

TILE = 128
PANEL = 1024
META = 16
F32 = jnp.float32
BF16 = jnp.bfloat16
NN = (((1,), (0,)), ((), ()))
NT = (((1,), (1,)), ((), ()))
TN = (((0,), (0,)), ((), ()))

noise_var = 0.5


def iota(shape, dim):
    return lax.broadcasted_iota(jnp.int32, shape, dim)


def one_hot(cond):
    return jnp.where(cond, 1.0, 0.0).astype(BF16)


def dot(left, right, dims=NN):
    return lax.dot_general(left, right, dims, preferred_element_type=F32)


def split(value):
    high = value.astype(BF16)
    return high, (value - high.astype(F32)).astype(BF16)


def dot_split(left, right, dims=NN):
    return dot(left[0], right[0], dims) + (
        dot(left[0], right[1], dims) + dot(left[1], right[0], dims)
    )


def half_norms(feats):
    wide = feats.astype(F32)
    return 0.5 * jnp.sum(wide * wide, axis=1, keepdims=True)


def as_row(column):
    rows = column.shape[0]
    return jnp.broadcast_to(column, (rows, TILE)).T[:1, :]


def rbf(left, left_half, right, right_half_row):
    cross = dot(left, right, NT)
    return jnp.exp(jnp.minimum(cross - left_half - right_half_row, 0.0))


def feature_kernel(
    share, row_count, pos_ref, img_ref, win_ref, bias_ref, wout_ref, scale_ref, out_ref, acc_ref
):
    step = pl.program_id(0)
    preact = dot(img_ref[...], win_ref[...]) + bias_ref[...]
    hidden = 0.5 * preact * (1.0 + jnp.tanh(0.7978845608 * (preact + 0.044715 * preact * preact * preact)))
    part = dot(hidden.astype(BF16), wout_ref[...])

    @pl.when(step == 0)
    def _():
        acc_ref[...] = part

    @pl.when(step > 0)
    def _():
        acc_ref[...] += part

    @pl.when(step == pl.num_programs(0) - 1)
    def _():
        images = row_count * share
        feats = (acc_ref[...] * scale_ref[...]).astype(BF16)
        place = pos_ref[...]
        tile = place // TILE
        group = tile % row_count
        member = iota((row_count, images), 0) == group
        before = one_hot(iota((images, images), 0) < iota((images, images), 1))
        rank = dot(one_hot(member), before)
        target = jnp.where(member, rank + (share * iota((row_count, images), 0)).astype(F32), 0.0)
        target = jnp.sum(target, axis=0, keepdims=True).astype(jnp.int32)
        order = one_hot(iota((images, images), 0) == target)
        sorted_feats = dot(order, feats).astype(BF16)
        meta_row = iota((META, images), 0)
        meta = jnp.where(meta_row == 0, tile // row_count, jnp.where(meta_row == 1, place % TILE, 0))
        meta = meta.astype(F32).astype(BF16)
        lane = iota((TILE, images), 0) % share
        for r in range(row_count):
            out_ref[r, :share, :] = sorted_feats[r * share : (r + 1) * share, :]
            sel = one_hot(lane + r * share == target)
            spread = dot(meta, sel, NT).astype(BF16)
            out_ref[r, share:, :TILE] = spread
            out_ref[r, share:, TILE:] = jnp.zeros((META, out_ref.shape[2] - TILE), BF16)


def make_features(images, weight_in, bias_in, weight_out, feature_scale, position, row_count):
    rows, din = images.shape
    hid, feat = weight_out.shape
    share = rows // row_count
    block = 512
    return pl.pallas_call(
        functools.partial(feature_kernel, share, row_count),
        out_shape=jax.ShapeDtypeStruct((row_count, share + META, feat), BF16),
        grid=(hid // block,),
        in_specs=[
            pl.BlockSpec((1, rows), lambda i: (0, 0)),
            pl.BlockSpec((rows, din), lambda i: (0, 0)),
            pl.BlockSpec((din, block), lambda i: (0, i)),
            pl.BlockSpec((1, block), lambda i: (0, i)),
            pl.BlockSpec((block, feat), lambda i: (i, 0)),
            pl.BlockSpec((1, feat), lambda i: (0, 0)),
        ],
        out_specs=pl.BlockSpec((row_count, share + META, feat), lambda i: (0, 0, 0)),
        scratch_shapes=[pltpu.VMEM((rows, feat), F32)],
        compiler_params=pltpu.CompilerParams(vmem_limit_bytes=32 << 20),
        name="features",
    )(
        position.reshape(1, rows),
        images,
        weight_in,
        bias_in.reshape(1, hid),
        weight_out,
        feature_scale.reshape(1, feat),
    )


def read_slots(block_ref, lead, share, group):
    per = TILE // share
    lane = iota((META, TILE), 1) // share
    meta = None
    for j in range(per):
        piece = block_ref[lead + (group * per + j, slice(share, share + META), slice(0, TILE))].astype(F32)
        meta = piece if meta is None else jnp.where(lane == j, piece, meta)
    return (meta[0:1, :] * TILE + meta[1:2, :]).astype(jnp.int32)


def gather_rows(block_ref, lead, share, group):
    per = TILE // share
    return jnp.concatenate(
        [block_ref[lead + (group * per + j, slice(0, share), slice(None))] for j in range(per)], axis=0
    )


def lead_kernel(share, recv_ref, *out_refs):
    groups = recv_ref.shape[0] * share // TILE
    slots = [read_slots(recv_ref, (), share, g) for g in range(groups)]
    rows = jnp.concatenate([gather_rows(recv_ref, (), share, g) for g in range(groups)], axis=0)
    for t, out_ref in enumerate(out_refs):
        pick = jnp.concatenate(
            [one_hot(iota((TILE, TILE), 0) + t * TILE == s) for s in slots], axis=1
        )
        out_ref[...] = dot(pick, rows).astype(BF16)


def make_lead(received, share, lead_tiles):
    feat = received.shape[2]
    shape = jax.ShapeDtypeStruct((TILE, feat), BF16)
    return pl.pallas_call(
        functools.partial(lead_kernel, share), out_shape=[shape] * lead_tiles, name="lead"
    )(received)


def diag_inverse(block):
    size, width = block.shape[0], 8
    count = size // width
    sub = iota((width, size), 0)
    lane = iota((width, size), 1)
    left = [block[q * width : (q + 1) * width, :] for q in range(count)]
    right = [jnp.where(lane == sub + q * width, 1.0, 0.0).astype(F32) for q in range(count)]
    out = []
    for g in range(count):
        base = g * width
        pivot_l, pivot_r = left[g], right[g]
        cols = [
            jnp.broadcast_to(pivot_l[:, base + k : base + k + 1], (width, size)) for k in range(width)
        ]
        diag = jnp.ones((width, size), F32)
        for i in range(width):
            own = jnp.broadcast_to(cols[i][i : i + 1, :], (width, size))
            diag = jnp.where(sub == i, own, diag)
            factor = jnp.where(sub > i, cols[i] / own, 0.0)
            for k in range(i + 1, width):
                cols[k] = cols[k] - factor * jnp.broadcast_to(cols[k][i : i + 1, :], (width, size))
            pivot_l = pivot_l - factor * jnp.broadcast_to(pivot_l[i : i + 1, :], (width, size))
            pivot_r = pivot_r - factor * jnp.broadcast_to(pivot_r[i : i + 1, :], (width, size))
        scale = lax.rsqrt(diag)
        pivot_l, pivot_r = pivot_l * scale, pivot_r * scale
        out.append(pivot_r)
        if g + 1 < count:
            turned = pivot_l.T
            for q in range(g + 1, count):
                rest_l, rest_r = left[q], right[q]
                for i in range(width):
                    c = jnp.broadcast_to(turned[q * width : (q + 1) * width, i : i + 1], (width, size))
                    rest_l = rest_l - c * jnp.broadcast_to(pivot_l[i : i + 1, :], (width, size))
                    rest_r = rest_r - c * jnp.broadcast_to(pivot_r[i : i + 1, :], (width, size))
                left[q], right[q] = rest_l, rest_r
    return jnp.concatenate(out, axis=0)


def chol_kernel(cols_ref, out_ref, work_ref, high_ref, low_ref):
    blocks = PANEL // TILE
    feats = cols_ref[...]
    half = half_norms(feats)
    half_row = as_row(half)
    eye = iota((TILE, PANEL), 0) - iota((TILE, PANEL), 1)
    for k in range(blocks):
        rows = slice(k * TILE, (k + 1) * TILE)
        block = rbf(feats[rows], half[rows], feats, half_row)
        work_ref[rows, :] = block + jnp.where(eye == -k * TILE, noise_var, 0.0)
    lane = iota((TILE, PANEL), 1)

    def step(k, carry):
        base = pl.multiple_of(k * TILE, TILE)
        inverse = diag_inverse(work_ref[pl.ds(base, TILE), pl.ds(base, TILE)])
        work_ref[pl.ds(base, TILE), pl.ds(base, TILE)] = jnp.where(
            iota((TILE, TILE), 0) == iota((TILE, TILE), 1), 1.0, 0.0
        )
        row = dot_split(split(inverse), split(work_ref[pl.ds(base, TILE), :]))
        out_ref[pl.ds(base, TILE), :] = jnp.where(lane < base + TILE, row, 0.0)
        high, low = split(row)
        high_ref[...] = high
        low_ref[...] = low

        def trail(i, inner):
            start = pl.multiple_of(i * TILE, TILE)
            work_ref[pl.ds(start, TILE), pl.ds(base, TILE)] = jnp.zeros((TILE, TILE), F32)
            lower = (high_ref[:, pl.ds(start, TILE)], low_ref[:, pl.ds(start, TILE)])
            work_ref[pl.ds(start, TILE), :] -= dot_split(lower, (high_ref[...], low_ref[...]), TN)
            return inner

        lax.fori_loop(k + 1, blocks, trail, 0)
        return carry

    lax.fori_loop(0, blocks, step, 0)


def make_inverse(columns):
    return pl.pallas_call(
        chol_kernel,
        out_shape=jax.ShapeDtypeStruct((PANEL, PANEL), F32),
        scratch_shapes=[
            pltpu.VMEM((PANEL, PANEL), F32),
            pltpu.VMEM((TILE, PANEL), BF16),
            pltpu.VMEM((TILE, PANEL), BF16),
        ],
        compiler_params=pltpu.CompilerParams(vmem_limit_bytes=40 << 20),
        name="cholesky",
    )(columns)


def panel_kernel(
    share, row_count, col_count, rows_blk, place_ref, recv_ref, cols_ref, next_ref, inv_ref,
    panel_ref, update_ref, feats_ref, slots_ref, high_ref, low_ref, half_ref, own_ref, own_half_ref,
):
    step = pl.program_id(0)
    row_index, col_index = place_ref[0], place_ref[1]
    col_tiles = PANEL // TILE // col_count
    width = col_tiles * TILE
    parts, per_part = recv_ref.shape[0], recv_ref.shape[1]
    groups = per_part * share // TILE
    total = parts * groups

    @pl.when(step == 0)
    def _():
        for p in range(parts):
            for g in range(groups):
                q = p * groups + g
                slots_ref[:, q * TILE : (q + 1) * TILE] = jnp.broadcast_to(
                    read_slots(recv_ref, (p,), share, g), (8, TILE)
                )
                feats_ref[q * TILE : (q + 1) * TILE, :] = gather_rows(recv_ref, (p,), share, g)
        half_row = as_row(half_norms(cols_ref[...]))
        half_ref[...] = jnp.broadcast_to(half_row, (8, PANEL))
        inverse = split(inv_ref[...])
        own = []
        for t in range(col_tiles):
            start = pl.multiple_of((t * col_count + col_index) * TILE, TILE)
            own_ref[t * TILE : (t + 1) * TILE, :] = next_ref[pl.ds(start, TILE), :]
            own.append(inv_ref[pl.ds(start, TILE), :])
        own_feats = own_ref[...]
        own_half = half_norms(own_feats)
        own_half_ref[...] = jnp.broadcast_to(as_row(own_half), (8, width))
        cross = rbf(own_feats, own_half, cols_ref[...], half_row)
        solved = dot_split(split(dot_split(split(cross), inverse, NT)), inverse)
        right = jnp.concatenate(own + [solved], axis=0)
        high, low = split(right.T)
        high_ref[...] = high
        low_ref[...] = low

    def body(diagonal):
        slot = iota((rows_blk, TILE), 0) + step * rows_blk
        pick = jnp.concatenate(
            [one_hot(slot == slots_ref[0:1, q * TILE : (q + 1) * TILE]) for q in range(total)], axis=1
        )
        feats = dot(pick, feats_ref[...]).astype(BF16)
        half = half_norms(feats)
        kern = rbf(feats, half, cols_ref[...], half_ref[0:1, :])
        kern_next = rbf(feats, half, own_ref[...], own_half_ref[0:1, :])
        if diagonal:
            local = iota((rows_blk, 1), 0) + step * rows_blk
            place = (local // TILE * row_count + row_index) * TILE + local % TILE
            kern = kern + jnp.where(place == iota((rows_blk, PANEL), 1), noise_var, 0.0)
            index = iota((rows_blk, width), 1)
            column = PANEL + (index // TILE * col_count + col_index) * TILE + index % TILE
            kern_next = kern_next + jnp.where(place == column, noise_var, 0.0)
        result = dot_split(split(kern), (high_ref[...], low_ref[...]))
        update = kern_next - result[:, width:]
        for t in range(col_tiles):
            where = pl.ds(t, rows_blk, stride=col_tiles) if col_tiles > 1 else slice(None)
            panel_ref[where, :] = result[:, t * TILE : (t + 1) * TILE]
            update_ref[where, :] = update[:, t * TILE : (t + 1) * TILE]

    lead_rows = max(2 * PANEL // row_count, TILE)
    has_diag = step * rows_blk < lead_rows

    @pl.when(has_diag)
    def _():
        body(True)

    @pl.when(jnp.logical_not(has_diag))
    def _():
        body(False)


def make_outputs(received, columns, following, inverse, share, row_count, col_count):
    parts, per_part, _, feat = received.shape
    local_rows = parts * per_part * share
    col_tiles = PANEL // TILE // col_count
    width = col_tiles * TILE
    rows_blk = 256
    row_index = lax.axis_index("row")
    col_index = lax.axis_index("col")
    place = jnp.stack([row_index, col_index]).astype(jnp.int32)
    whole = lambda *shape: pl.BlockSpec(shape, lambda i, s: (0,) * len(shape), pipeline_mode=pl.Buffered(1))
    out = jax.ShapeDtypeStruct((local_rows * col_tiles, TILE), F32)
    out_spec = pl.BlockSpec((rows_blk * col_tiles, TILE), lambda i, s: (i, 0))
    return pl.pallas_call(
        functools.partial(panel_kernel, share, row_count, col_count, rows_blk),
        out_shape=[out, out],
        grid_spec=pltpu.PrefetchScalarGridSpec(
            num_scalar_prefetch=1,
            grid=(local_rows // rows_blk,),
            in_specs=[
                whole(*received.shape),
                whole(PANEL, feat),
                whole(*following.shape),
                whole(PANEL, PANEL),
            ],
            out_specs=[out_spec, out_spec],
            scratch_shapes=[
                pltpu.VMEM((local_rows, feat), BF16),
                pltpu.VMEM((8, local_rows), jnp.int32),
                pltpu.VMEM((PANEL, 2 * width), BF16),
                pltpu.VMEM((PANEL, 2 * width), BF16),
                pltpu.VMEM((8, PANEL), F32),
                pltpu.VMEM((width, feat), BF16),
                pltpu.VMEM((8, width), F32),
            ],
        ),
        compiler_params=pltpu.CompilerParams(vmem_limit_bytes=56 << 20),
        name="panels",
    )(place, received, columns, following, inverse)


def shift(value, axis, distance, size):
    return lax.ppermute(value, axis, [(i, (i + distance) % size) for i in range(size)])


def sum_over(value, axis, size):
    step = 1
    while step < size:
        value = value + lax.ppermute(value, axis, [(i, i ^ step) for i in range(size)])
        step *= 2
    return value


def per_device(images, weight_in, bias_in, weight_out, feature_scale, position):
    image_rows = images.shape[0]
    feat = weight_out.shape[1]
    row_count = lax.axis_size("row")
    col_count = lax.axis_size("col")
    share = image_rows // row_count
    lead_tiles = 2 * PANEL // (TILE * row_count)
    bucket = make_features(
        images, weight_in, bias_in, weight_out, feature_scale, position, row_count
    )
    received = lax.all_to_all(bucket, "row", split_axis=0, concat_axis=0, tiled=True)
    lead = make_lead(received, share, lead_tiles)
    columns = lax.all_gather(sum_over(lead[0], "col", col_count), "row", axis=0, tiled=True)
    received, columns, rest = lax.optimization_barrier((received, columns, lead[1:]))
    others = [shift(received, "col", d, col_count) for d in range(1, col_count)]
    every = jnp.stack([received] + others, axis=0)
    for tile in rest:
        more = lax.all_gather(sum_over(tile, "col", col_count), "row", axis=0, tiled=True)
        columns = jnp.concatenate([columns, more], axis=0)
    first, following = columns[:PANEL], columns[PANEL:]
    inverse = make_inverse(first)
    panel, update = make_outputs(every, first, following, inverse, share, row_count, col_count)
    shape_out = (image_rows * col_count // TILE, TILE, PANEL // TILE // col_count, TILE)
    return panel.reshape(shape_out), update.reshape(shape_out)


def solution(mesh):
    in_specs = (P(("row", "col"), None), P(), P(), P(), P(), P(("row", "col")))
    out_specs = (P(None, "row", None, "col"), P(None, "row", None, "col"))
    return jax.shard_map(
        per_device, mesh=mesh, in_specs=in_specs, out_specs=out_specs, check_vma=False
    )
```

time: 519 us -> 177 us (0.34); the launches traced: 509 us -> 175 us
  other arithmetic: 279 us -> 3.67 us
  Pallas kernels: 0 us -> 92.2 us
  matrix products: 82.9 us -> 0 us
  local copies, waits for them, and re-layouts: 69.2 us -> 8.26 us
  blocking collectives: 0 us -> 33.6 us
  between operations: 20.2 us -> 0.71 us
  waiting for transfers between devices: 45.5 us -> 27.1 us
    another operation x34 -> x2, other arithmetic: 265 us -> 1.92 us  [the longest x1 1.27 us: per_device(): every = jnp.stack([received] + others, axis=0)]
    pallas_call x0 -> x4, Pallas kernels: none -> 92.2 us  [the longest x1 61.4 us: make_inverse(): pl.pallas_call(chol_kernel, out_shape=jax.ShapeDtypeStruct((PANEL, PANEL)...]
    another operation x59 -> x0, matrix products: 48.8 us -> none  [the longest x14 23.5 us: per_device(): factor = jnp.linalg.cholesky(block_diag)]
    dot_general x7 -> x0, matrix products: 34.1 us -> none  [the longest x4 14.8 us: kernel_block(): jnp.dot(left_feats, right_feats.T, preferred_element_type=jnp.float32)]
    another operation x41 -> x0, local copies, waits for them, and re-layouts: 30.6 us -> none  [the longest x29 28 us: per_device(): jax.scipy.linalg.solve_triangular(factor, picker, lower=True, trans=1)]
    ppermute x0 -> x7, waiting for transfers between devices: none -> 27.1 us  [the longest x4 27.1 us: sum_over(): lax.ppermute(value, axis, [(i, i ^ step) for i in range(size)])]
    all_to_all x2 -> x0, waiting for transfers between devices: 23.3 us -> none  [the longest x1 23.3 us: per_device(): lax.all_to_all(widened, ('row', 'col'), split_axis=0, concat_axis=0, tile...]
    all_gather x0 -> x2, blocking collectives: none -> 23.1 us  [the longest x1 12.4 us: per_device(): lax.all_gather(sum_over(lead[0], 'col', col_count), 'row', axis=0, tiled=...]
  transfers between devices with their start and end apart: 3 -> 7, of which waited for: 2 -> 3; matrix products, arithmetic and copies ran while one was open for 2% -> 1% of each run, Pallas kernels for 0% -> 35%
where the time goes in v1:
time: 177 us; the launch traced here: 175 us
  Pallas kernels  92.2 us (52%)
  blocking collectives  33.6 us (19%)
  waiting for transfers between devices  27.1 us (15%)
  starting transfers between devices  9.51 us (5%)
  local copies, waits for them, and re-layouts  8.26 us (5%)
  other arithmetic  3.67 us (2%)
    pallas_call x1, Pallas kernels, make_inverse(): pl.pallas_call(chol_kernel, out_shape=jax.ShapeDtypeStruct((PANEL, PANEL)...  61.4 us
    ppermute x4, waiting for transfers between devices, sum_over(): lax.ppermute(value, axis, [(i, i ^ step) for i in range(size)])  27.1 us
    pallas_call x1, Pallas kernels, make_outputs(): pl.pallas_call(functools.partial(panel_kernel, share, row_count, col_coun...  24.1 us
    all_gather x1, blocking collectives, per_device(): lax.all_gather(sum_over(lead[0], 'col', col_count), 'row', axis=0, tiled=...  12.4 us
    all_gather x1, blocking collectives, per_device(): lax.all_gather(sum_over(tile, 'col', col_count), 'row', axis=0, tiled=True)  10.7 us
    all_to_all x1, blocking collectives, per_device(): lax.all_to_all(bucket, 'row', split_axis=0, concat_axis=0, tiled=True)  10.4 us
    unnamed x18, local copies, waits for them, and re-layouts  8.26 us
    ppermute x3, starting transfers between devices, shift(): lax.ppermute(value, axis, [(i, (i + distance) % size) for i in range(size)])  5.34 us
  transfers between devices with their start and end apart: 7, of which 3 were waited for; matrix products, arithmetic and copies ran while one was open for 1% of the time, Pallas kernels for 35%

profile of v1, /device:TPU:11, one launch (start us, length us, event | category | flops | bytes accessed | tf_op | source)
XLA Modules:
  0.0 175.0 jit_solution(1170841810419598635)
XLA Ops:
  0.6 0.0 copy-start.2
  0.6 1.9 %copy-done.2 = bf16[768,2048]{1,0:T(8,128)(2,1)S(1)} copy-done((bf16[768,2048]{1,0:T(8,128)(2,1)S(1)}, bf16[768,2048]{1,0:T(8,128)(2,1)}, u32[]{:S(2)}) %copy-start.2) | copy-done | bytes 3145752
  2.5 0.0 copy-start.3
  2.5 1.2 copy-done.3
  3.7 0.0 copy-start.4
  3.7 1.1 copy-done.4
  4.9 0.0 copy-start.5
  4.9 0.7 copy-done.5
  5.6 0.0 copy-start.6
  5.6 0.7 copy-done.6
  6.3 0.0 copy-start.7
  6.3 0.7 copy-done.7
  6.9 4.7 %features.1 = bf16[8,80,256]{2,1,0:T(8,128)(2,1)S(1)} custom-call(s32[1,512]{1,0:T(1,128)S(1)} %bitcast.12, bf16[512,768]{1,0:T(8,128)(2,1)S(1)} %copy-done.4, bf16[768,2048]{1,0:T(8,128)(2,1)S(1)} %copy-done.2, f32[1,2048]{1,0:T(1,128)S(1)} %bitcast.11, bf16[2048,256]{1,0:T(8,128)(2,1)S(1)} %copy-done.3, f32[1,256]{1,0:T(1,128)S(1)} %bitcast.13), custom_call_target="tpu_custom_call" | custom-call | tf_op jit(solution)/shard_map/features/pallas_call | solution.py:107
  11.7 10.4 %all_to_all.5.recv_ref = bf16[8,80,256]{2,1,0:T(8,128)(2,1)} all-to-all(bf16[8,80,256]{2,1,0:T(8,128)(2,1)S(1)} %features.1), channel_id=1, replica_groups=mesh['row'=8,'col'=4] {'row'}, dimensions={0} | all-to-all | bytes 655360 | tf_op jit(solution)/shard_map/all_to_all | solution.py:394
  22.1 0.0 copy-start.8
  22.1 1.9 %lead.1 = (bf16[128,256]{1,0:T(8,128)(2,1)}, bf16[128,256]{1,0:T(8,128)(2,1)}) custom-call(bf16[8,80,256]{2,1,0:T(8,128)(2,1)} %all_to_all.5.recv_ref), custom_call_target="tpu_custom_call" | custom-call | tf_op jit(solution)/shard_map/lead/pallas_call | solution.py:164
  24.0 0.2 collective-permute-start
  24.2 3.2 %collective-permute-done = bf16[128,256]{1,0:T(8,128)(2,1)S(1)} collective-permute-done((bf16[128,256]{1,0:T(8,128)(2,1)}, bf16[128,256]{1,0:T(8,128)(2,1)S(1)}, u32[]{:S(2)}, u32[]{:S(2)}) %collective-permute-start) | collective-permute-done | bytes 65568 | tf_op jit(solution)/shard_map/ppermute | solution.py:379
  27.4 0.9 add.12
  28.2 2.4 %collective-permute-start.1 = (bf16[128,256]{1,0:T(8,128)(2,1)S(1)}, bf16[128,256]{1,0:T(8,128)(2,1)S(1)}, u32[]{:S(2)}, u32[]{:S(2)}) collective-permute-start(bf16[128,256]{1,0:T(8,128)(2,1)S(1)} %add.12), channel_id=1, source_target_pairs={{0,2},{1,3},{2,0},{3,1},{4,6},{5,7},{6,4},{7,5},{8,10},{9,11},{10,... | collective-permute-start | bytes 196616 | tf_op jit(solution)/shard_map/ppermute | solution.py:379
  30.6 1.8 %collective-permute-done.1 = bf16[128,256]{1,0:T(8,128)(2,1)S(1)} collective-permute-done((bf16[128,256]{1,0:T(8,128)(2,1)S(1)}, bf16[128,256]{1,0:T(8,128)(2,1)S(1)}, u32[]{:S(2)}, u32[]{:S(2)}) %collective-permute-start.1) | collective-permute-done | bytes 65568 | tf_op jit(solution)/shard_map/ppermute | solution.py:379
  32.4 12.4 %all_gather.6.cols_ref = bf16[1024,256]{1,0:T(8,128)(2,1)S(1)} all-gather(bf16[128,256]{1,0:T(8,128)(2,1)S(1)} %add.13), channel_id=1, replica_groups=mesh['row'=8,'col'=4] {'row'}, dimensions={0}, use_global_device_ids=true | all-gather | bytes 589824 | tf_op jit(solution)/shard_map/all_gather | solution.py:396
  44.9 0.0 copy-start.1
  44.9 0.0 copy-done.8
  44.9 0.2 collective-permute-start.4
  45.1 2.8 %collective-permute-start.3 = (bf16[8,80,256]{2,1,0:T(8,128)(2,1)S(1)}, bf16[8,80,256]{2,1,0:T(8,128)(2,1)S(1)}, u32[]{:S(2)}, u32[]{:S(2)}) collective-permute-start(bf16[8,80,256]{2,1,0:T(8,128)(2,1)S(1)} %copy-done.8), channel_id=1, source_target_pairs={{0,2},{1,3},{2,0},{3,1},{4,6},{5,7},{6,4},{7,5},{8,10},{9,11},{10,... | collective-permute-start | bytes 983048 | tf_op jit(solution)/shard_map/ppermute | solution.py:373
  47.9 2.3 %collective-permute-start.2 = (bf16[8,80,256]{2,1,0:T(8,128)(2,1)S(1)}, bf16[8,80,256]{2,1,0:T(8,128)(2,1)S(1)}, u32[]{:S(2)}, u32[]{:S(2)}) collective-permute-start(bf16[8,80,256]{2,1,0:T(8,128)(2,1)S(1)} %copy-done.8), channel_id=1, source_target_pairs={{0,1},{1,2},{2,3},{3,0},{4,5},{5,6},{6,7},{7,4},{8,9},{9,10},{10,1... | collective-permute-start | bytes 983048 | tf_op jit(solution)/shard_map/ppermute | solution.py:373
  50.2 0.0 collective-permute-start.5
  50.2 22.1 %collective-permute-done.5 = bf16[128,256]{1,0:T(8,128)(2,1)S(1)} collective-permute-done((bf16[128,256]{1,0:T(8,128)(2,1)}, bf16[128,256]{1,0:T(8,128)(2,1)S(1)}, u32[]{:S(2)}, u32[]{:S(2)}) %collective-permute-start.5) | collective-permute-done | bytes 65568 | tf_op jit(solution)/shard_map/ppermute | solution.py:379
  72.4 0.9 add.14
  73.2 1.6 collective-permute-start.6
  74.8 0.6 pad_add_fusion.place_ref
  75.5 61.4 %cholesky.1.inv_ref = f32[1024,1024]{1,0:T(8,128)S(1)} custom-call(bf16[1024,256]{1,0:T(8,128)(2,1)S(1)} %all_gather.6.cols_ref), custom_call_target="tpu_custom_call" | custom-call | tf_op jit(solution)/shard_map/cholesky/pallas_call | solution.py:245
  136.9 0.0 copy-done.1
  136.9 0.0 copy-start
  136.9 2.0 %copy-done = f32[1024,1024]{1,0:T(8,128)} copy-done((f32[1024,1024]{1,0:T(8,128)}, f32[1024,1024]{1,0:T(8,128)S(1)}, u32[]{:S(2)}) %copy-start) | copy-done | bytes 4194328
  138.9 0.0 collective-permute-done.6
  138.9 10.7 %all_gather.7.next_ref = bf16[1024,256]{1,0:T(8,128)(2,1)} all-gather(bf16[128,256]{1,0:T(8,128)(2,1)S(1)} %add.15), channel_id=1, replica_groups=mesh['row'=8,'col'=4] {'row'}, dimensions={0}, use_global_device_ids=true | all-gather | bytes 589824 | tf_op jit(solution)/shard_map/all_gather | solution.py:401
  149.6 0.0 collective-permute-done.4
  149.6 0.0 collective-permute-done.3
  149.6 0.0 collective-permute-done.2
  149.6 1.3 pad_maximum_fusion.recv_ref
  150.9 24.1 %panels.1 = (f32[4096,128]{1,0:T(8,128)}, f32[4096,128]{1,0:T(8,128)}) custom-call(s32[2]{0:T(128)} %pad_add_fusion.place_ref, bf16[4,8,80,256]{3,2,1,0:T(8,128)(2,1)} %pad_maximum_fusion.recv_ref, bf16[1024,256]{1,0:T(8,128)(2,1)} %copy-done.1, bf16[1024,256]{1,0:T(8,128)(2,1)} %all_gather.7.next_ref, f32[1024,1024]{1,0:T(8,128)} %copy-done), custom_call_target="tpu_custom_call" | custom-call | tf_op jit(solution)/shard_map/panels/pallas_call | solution.py:344
  (2 shorter events, 0.0 us)
Async XLA Ops:
  0.6 1.9 %copy-start.2 = (bf16[768,2048]{1,0:T(8,128)(2,1)S(1)}, bf16[768,2048]{1,0:T(8,128)(2,1)}, u32[]{:S(2)}) copy-start(bf16[768,2048]{1,0:T(8,128)(2,1)} %win_ref.1) | copy-start | bytes 9437188
  2.5 1.2 copy-start.3
  3.7 1.1 copy-start.4
  4.9 0.7 copy-start.5
  5.6 0.7 copy-start.6
  6.3 0.7 copy-start.7
  22.1 22.7 %copy-start.8 = (bf16[8,80,256]{2,1,0:T(8,128)(2,1)S(1)}, bf16[8,80,256]{2,1,0:T(8,128)(2,1)}, u32[]{:S(2)}) copy-start(bf16[8,80,256]{2,1,0:T(8,128)(2,1)} %all_to_all.5.recv_ref) | copy-start | bytes 983044
  24.0 3.3 %collective-permute-start = (bf16[128,256]{1,0:T(8,128)(2,1)}, bf16[128,256]{1,0:T(8,128)(2,1)S(1)}, u32[]{:S(2)}, u32[]{:S(2)}) collective-permute-start(bf16[128,256]{1,0:T(8,128)(2,1)} %get-tuple-element.9), channel_id=1, source_target_pairs={{0,1},{1,0},{2,3},{3,2},{4,5},{5,4},{6,7},{7,6},{8,9},{9,8},{10,11... | collective-permute-start | bytes 196616 | tf_op jit(solution)/shard_map/ppermute | solution.py:379
  28.2 4.2 %collective-permute-start.1 = (bf16[128,256]{1,0:T(8,128)(2,1)S(1)}, bf16[128,256]{1,0:T(8,128)(2,1)S(1)}, u32[]{:S(2)}, u32[]{:S(2)}) collective-permute-start(bf16[128,256]{1,0:T(8,128)(2,1)S(1)} %add.12), channel_id=1, source_target_pairs={{0,2},{1,3},{2,0},{3,1},{4,6},{5,7},{6,4},{7,5},{8,10},{9,11},{10,... | collective-permute-start | bytes 196616 | tf_op jit(solution)/shard_map/ppermute | solution.py:379
  44.9 92.1 %copy-start.1 = (bf16[1024,256]{1,0:T(8,128)(2,1)}, bf16[1024,256]{1,0:T(8,128)(2,1)S(1)}, u32[]{:S(2)}) copy-start(bf16[1024,256]{1,0:T(8,128)(2,1)S(1)} %all_gather.6.cols_ref) | copy-start | bytes 1572868
  44.9 104.7 %collective-permute-start.4 = (bf16[8,80,256]{2,1,0:T(8,128)(2,1)S(1)}, bf16[8,80,256]{2,1,0:T(8,128)(2,1)S(1)}, u32[]{:S(2)}, u32[]{:S(2)}) collective-permute-start(bf16[8,80,256]{2,1,0:T(8,128)(2,1)S(1)} %copy-done.8), channel_id=1, source_target_pairs={{0,3},{1,0},{2,1},{3,2},{4,7},{5,4},{6,5},{7,6},{8,11},{9,8},{10,9... | collective-permute-start | bytes 983048 | tf_op jit(solution)/shard_map/ppermute | solution.py:373
  45.1 104.5 %collective-permute-start.3 = (bf16[8,80,256]{2,1,0:T(8,128)(2,1)S(1)}, bf16[8,80,256]{2,1,0:T(8,128)(2,1)S(1)}, u32[]{:S(2)}, u32[]{:S(2)}) collective-permute-start(bf16[8,80,256]{2,1,0:T(8,128)(2,1)S(1)} %copy-done.8), channel_id=1, source_target_pairs={{0,2},{1,3},{2,0},{3,1},{4,6},{5,7},{6,4},{7,5},{8,10},{9,11},{10,... | collective-permute-start | bytes 983048 | tf_op jit(solution)/shard_map/ppermute | solution.py:373
  47.9 101.7 %collective-permute-start.2 = (bf16[8,80,256]{2,1,0:T(8,128)(2,1)S(1)}, bf16[8,80,256]{2,1,0:T(8,128)(2,1)S(1)}, u32[]{:S(2)}, u32[]{:S(2)}) collective-permute-start(bf16[8,80,256]{2,1,0:T(8,128)(2,1)S(1)} %copy-done.8), channel_id=1, source_target_pairs={{0,1},{1,2},{2,3},{3,0},{4,5},{5,6},{6,7},{7,4},{8,9},{9,10},{10,1... | collective-permute-start | bytes 983048 | tf_op jit(solution)/shard_map/ppermute | solution.py:373
  50.2 22.1 %collective-permute-start.5 = (bf16[128,256]{1,0:T(8,128)(2,1)}, bf16[128,256]{1,0:T(8,128)(2,1)S(1)}, u32[]{:S(2)}, u32[]{:S(2)}) collective-permute-start(bf16[128,256]{1,0:T(8,128)(2,1)} %get-tuple-element.13), channel_id=1, source_target_pairs={{0,1},{1,0},{2,3},{3,2},{4,5},{5,4},{6,7},{7,6},{8,9},{9,8},{10,11... | collective-permute-start | bytes 196616 | tf_op jit(solution)/shard_map/ppermute | solution.py:379
  73.2 65.7 %collective-permute-start.6 = (bf16[128,256]{1,0:T(8,128)(2,1)S(1)}, bf16[128,256]{1,0:T(8,128)(2,1)S(1)}, u32[]{:S(2)}, u32[]{:S(2)}) collective-permute-start(bf16[128,256]{1,0:T(8,128)(2,1)S(1)} %add.14), channel_id=1, source_target_pairs={{0,2},{1,3},{2,0},{3,1},{4,6},{5,7},{6,4},{7,5},{8,10},{9,11},{10,... | collective-permute-start | bytes 196616 | tf_op jit(solution)/shard_map/ppermute | solution.py:379
  136.9 2.0 %copy-start = (f32[1024,1024]{1,0:T(8,128)}, f32[1024,1024]{1,0:T(8,128)S(1)}, u32[]{:S(2)}) copy-start(f32[1024,1024]{1,0:T(8,128)S(1)} %cholesky.1.inv_ref) | copy-start | bytes 12582916

commit v2 on v1

--- a/solution.py
+++ b/solution.py
@@ -104,6 +104,14 @@
     hid, feat = weight_out.shape
     share = rows // row_count
     block = 512
+    operands = (
+        position.reshape(1, rows),
+        images,
+        weight_in,
+        bias_in.reshape(1, hid),
+        weight_out,
+        feature_scale.reshape(1, feat),
+    )
     return pl.pallas_call(
         functools.partial(feature_kernel, share, row_count),
         out_shape=jax.ShapeDtypeStruct((row_count, share + META, feat), BF16),
@@ -120,14 +128,7 @@
         scratch_shapes=[pltpu.VMEM((rows, feat), F32)],
         compiler_params=pltpu.CompilerParams(vmem_limit_bytes=32 << 20),
         name="features",
-    )(
-        position.reshape(1, rows),
-        images,
-        weight_in,
-        bias_in.reshape(1, hid),
-        weight_out,
-        feature_scale.reshape(1, feat),
-    )
+    )(*[pltpu.with_memory_space_constraint(x, pltpu.HBM) for x in operands])
 
 
 def read_slots(block_ref, lead, share, group):
@@ -250,21 +251,21 @@
             pltpu.VMEM((TILE, PANEL), BF16),
             pltpu.VMEM((TILE, PANEL), BF16),
         ],
-        compiler_params=pltpu.CompilerParams(vmem_limit_bytes=40 << 20),
+        compiler_params=pltpu.CompilerParams(vmem_limit_bytes=24 << 20),
+        cost_estimate=pl.CostEstimate(flops=40 * 10**9, transcendentals=1 << 20, bytes_accessed=5 << 20),
         name="cholesky",
     )(columns)
 
 
-def panel_kernel(
-    share, row_count, col_count, rows_blk, place_ref, recv_ref, cols_ref, next_ref, inv_ref,
-    panel_ref, update_ref, feats_ref, slots_ref, high_ref, low_ref, half_ref, own_ref, own_half_ref,
-):
+def panel_kernel(share, row_count, col_count, rows_blk, parts, pieces, place_ref, *refs):
+    recv_refs, next_refs = refs[:parts], refs[parts : parts + pieces]
+    (cols_ref, inv_ref, panel_ref, update_ref, feats_ref, slots_ref, high_ref, low_ref, half_ref,
+     own_ref, own_half_ref) = refs[parts + pieces :]
     step = pl.program_id(0)
     row_index, col_index = place_ref[0], place_ref[1]
     col_tiles = PANEL // TILE // col_count
     width = col_tiles * TILE
-    parts, per_part = recv_ref.shape[0], recv_ref.shape[1]
-    groups = per_part * share // TILE
+    groups = recv_refs[0].shape[0] * share // TILE
     total = parts * groups
 
     @pl.when(step == 0)
@@ -273,17 +274,22 @@
             for g in range(groups):
                 q = p * groups + g
                 slots_ref[:, q * TILE : (q + 1) * TILE] = jnp.broadcast_to(
-                    read_slots(recv_ref, (p,), share, g), (8, TILE)
+                    read_slots(recv_refs[p], (), share, g), (8, TILE)
                 )
-                feats_ref[q * TILE : (q + 1) * TILE, :] = gather_rows(recv_ref, (p,), share, g)
+                feats_ref[q * TILE : (q + 1) * TILE, :] = gather_rows(recv_refs[p], (), share, g)
         half_row = as_row(half_norms(cols_ref[...]))
         half_ref[...] = jnp.broadcast_to(half_row, (8, PANEL))
         inverse = split(inv_ref[...])
         own = []
         for t in range(col_tiles):
-            start = pl.multiple_of((t * col_count + col_index) * TILE, TILE)
-            own_ref[t * TILE : (t + 1) * TILE, :] = next_ref[pl.ds(start, TILE), :]
-            own.append(inv_ref[pl.ds(start, TILE), :])
+            tile = t * col_count + col_index
+            for n, next_ref in enumerate(next_refs):
+
+                @pl.when(place_ref[2 + n] == tile)
+                def _():
+                    own_ref[t * TILE : (t + 1) * TILE, :] = next_ref[...]
+
+            own.append(inv_ref[pl.ds(pl.multiple_of(tile * TILE, TILE), TILE), :])
         own_feats = own_ref[...]
         own_half = half_norms(own_feats)
         own_half_ref[...] = jnp.broadcast_to(as_row(own_half), (8, width))
@@ -329,30 +335,23 @@
         body(False)
 
 
-def make_outputs(received, columns, following, inverse, share, row_count, col_count):
-    parts, per_part, _, feat = received.shape
-    local_rows = parts * per_part * share
+def make_outputs(parts, pieces, piece_tiles, columns, inverse, share, row_count, col_count):
+    feat = columns.shape[1]
+    local_rows = len(parts) * parts[0].shape[0] * share
     col_tiles = PANEL // TILE // col_count
     width = col_tiles * TILE
     rows_blk = 256
-    row_index = lax.axis_index("row")
-    col_index = lax.axis_index("col")
-    place = jnp.stack([row_index, col_index]).astype(jnp.int32)
-    whole = lambda *shape: pl.BlockSpec(shape, lambda i, s: (0,) * len(shape), pipeline_mode=pl.Buffered(1))
+    place = jnp.stack([lax.axis_index("row"), lax.axis_index("col")] + piece_tiles).astype(jnp.int32)
+    operands = (*parts, *pieces, columns, inverse)
     out = jax.ShapeDtypeStruct((local_rows * col_tiles, TILE), F32)
     out_spec = pl.BlockSpec((rows_blk * col_tiles, TILE), lambda i, s: (i, 0))
     return pl.pallas_call(
-        functools.partial(panel_kernel, share, row_count, col_count, rows_blk),
+        functools.partial(panel_kernel, share, row_count, col_count, rows_blk, len(parts), len(pieces)),
         out_shape=[out, out],
         grid_spec=pltpu.PrefetchScalarGridSpec(
             num_scalar_prefetch=1,
             grid=(local_rows // rows_blk,),
-            in_specs=[
-                whole(*received.shape),
-                whole(PANEL, feat),
-                whole(*following.shape),
-                whole(PANEL, PANEL),
-            ],
+            in_specs=[pl.BlockSpec(memory_space=pltpu.VMEM)] * len(operands),
             out_specs=[out_spec, out_spec],
             scratch_shapes=[
                 pltpu.VMEM((local_rows, feat), BF16),
@@ -364,21 +363,40 @@
                 pltpu.VMEM((8, width), F32),
             ],
         ),
-        compiler_params=pltpu.CompilerParams(vmem_limit_bytes=56 << 20),
+        compiler_params=pltpu.CompilerParams(vmem_limit_bytes=36 << 20),
         name="panels",
-    )(place, received, columns, following, inverse)
+    )(place, *operands)
 
 
 def shift(value, axis, distance, size):
     return lax.ppermute(value, axis, [(i, (i + distance) % size) for i in range(size)])
+
+
+def exchange(value, axis, step, size):
+    return lax.ppermute(value, axis, [(i, i ^ step) for i in range(size)])
 
 
 def sum_over(value, axis, size):
     step = 1
     while step < size:
-        value = value + lax.ppermute(value, axis, [(i, i ^ step) for i in range(size)])
+        value = value + exchange(value, axis, step, size)
         step *= 2
     return value
+
+
+def next_tiles(tile, row_count, col_count):
+    turns = PANEL // TILE // col_count
+    row_index, col_index = lax.axis_index("row"), lax.axis_index("col")
+    pieces, piece_tiles = [], []
+    for turn in range(turns):
+        pairs = []
+        for r in range(row_count):
+            for c in range(col_count):
+                owner = c + col_count * ((r // col_count + turn) % turns)
+                pairs.append((owner * col_count + r % col_count, r * col_count + c))
+        pieces.append(lax.ppermute(tile, ("row", "col"), pairs))
+        piece_tiles.append(col_index + col_count * ((row_index // col_count + turn) % turns))
+    return pieces, piece_tiles
 
 
 def per_device(images, weight_in, bias_in, weight_out, feature_scale, position):
@@ -393,16 +411,21 @@
     )
     received = lax.all_to_all(bucket, "row", split_axis=0, concat_axis=0, tiled=True)
     lead = make_lead(received, share, lead_tiles)
-    columns = lax.all_gather(sum_over(lead[0], "col", col_count), "row", axis=0, tiled=True)
-    received, columns, rest = lax.optimization_barrier((received, columns, lead[1:]))
-    others = [shift(received, "col", d, col_count) for d in range(1, col_count)]
-    every = jnp.stack([received] + others, axis=0)
-    for tile in rest:
-        more = lax.all_gather(sum_over(tile, "col", col_count), "row", axis=0, tiled=True)
-        columns = jnp.concatenate([columns, more], axis=0)
-    first, following = columns[:PANEL], columns[PANEL:]
-    inverse = make_inverse(first)
-    panel, update = make_outputs(every, first, following, inverse, share, row_count, col_count)
+    first, rest = lax.optimization_barrier((sum_over(lead[0], "col", col_count), lead[1:]))
+    rest = [[tile] + [shift(tile, "col", d, col_count) for d in range(1, col_count)] for tile in rest]
+    columns = lax.all_gather(first, "row", axis=0, tiled=True)
+    rest = [sum(pieces[1:], pieces[0]) for pieces in rest]
+    columns, rest, received = lax.optimization_barrier((columns, rest, received))
+    if rest:
+        pieces, piece_tiles = next_tiles(rest[0], row_count, col_count)
+    else:
+        pieces = [columns[PANEL + t * TILE : PANEL + (t + 1) * TILE] for t in range(PANEL // TILE)]
+        piece_tiles = [jnp.int32(t) for t in range(PANEL // TILE)]
+    parts = [received] + [shift(received, "col", d, col_count) for d in range(1, col_count)]
+    inverse = make_inverse(columns[:PANEL])
+    panel, update = make_outputs(
+        parts, pieces, piece_tiles, columns[:PANEL], inverse, share, row_count, col_count
+    )
     shape_out = (image_rows * col_count // TILE, TILE, PANEL // TILE // col_count, TILE)
     return panel.reshape(shape_out), update.reshape(shape_out)
 

time: 177 us -> 142 us (0.80)
  the two profiles are of different devices: /device:TPU:11 before, /device:TPU:0 now
where the time goes in v2:
time: 142 us
  Pallas kernels  91.7 us (65%)
  blocking collectives  21.6 us (15%)
  starting transfers between devices  20.3 us (14%)
  waiting for transfers between devices  5.42 us (4%)
  other arithmetic  1.81 us (1%)
    pallas_call x1, Pallas kernels, make_inverse(): pl.pallas_call(chol_kernel, out_shape=jax.ShapeDtypeStruct((PANEL, PANEL)...  61.6 us
    pallas_call x1, Pallas kernels, make_outputs(): pl.pallas_call(functools.partial(panel_kernel, share, row_count, col_coun...  22 us
    ppermute x6, starting transfers between devices, shift(): lax.ppermute(value, axis, [(i, (i + distance) % size) for i in range(size)])  13.9 us
    all_to_all x1, blocking collectives, per_device(): lax.all_to_all(bucket, 'row', split_axis=0, concat_axis=0, tiled=True)  12.7 us
    all_gather x1, blocking collectives, per_device(): columns = lax.all_gather(first, 'row', axis=0, tiled=True)  8.9 us
    pallas_call x1, Pallas kernels, make_features(): pl.pallas_call(functools.partial(feature_kernel, share, row_count), out_s...  6.28 us
    ppermute x2, waiting for transfers between devices, exchange(): return lax.ppermute(value, axis, [(i, i ^ step) for i in range(size)])  5.4 us
    ppermute x2, starting transfers between devices, exchange(): return lax.ppermute(value, axis, [(i, i ^ step) for i in range(size)])  4.23 us
  transfers between devices with their start and end apart: 10, of which 2 were waited for; matrix products, arithmetic and copies ran while one was open for 0% of the time, Pallas kernels for 43%

profile of v2, /device:TPU:0, one launch (start us, length us, event | category | flops | bytes accessed | tf_op | source)
XLA Modules:
  0.0 141.6 jit_solution(14101736853890199163)
XLA Ops:
  0.6 6.3 %features.1 = bf16[8,80,256]{2,1,0:T(8,128)(2,1)S(1)} custom-call(s32[1,512]{1,0:T(1,128)} %bitcast.10, bf16[512,768]{1,0:T(8,128)(2,1)} %img_ref.1, bf16[768,2048]{1,0:T(8,128)(2,1)} %win_ref.1, f32[1,2048]{1,0:T(1,128)} %bitcast.9, bf16[2048,256]{1,0:T(8,128)(2,1)} %wout_ref.1, f32[1,256]{1,0:T(1,128)} %bitcast.11), custom_call_target="tpu_custom_call" | custom-call | tf_op jit(solution)/shard_map/features/pallas_call | solution.py:115
  6.9 12.7 %all_to_all.5.recv_ref.refs_0_ = bf16[8,80,256]{2,1,0:T(8,128)(2,1)} all-to-all(bf16[8,80,256]{2,1,0:T(8,128)(2,1)S(1)} %features.1), channel_id=1, replica_groups=mesh['row'=8,'col'=4] {'row'}, dimensions={0} | all-to-all | bytes 655360 | tf_op jit(solution)/shard_map/all_to_all | solution.py:412
  19.6 1.8 %lead.1 = (bf16[128,256]{1,0:T(8,128)(2,1)}, bf16[128,256]{1,0:T(8,128)(2,1)}) custom-call(bf16[8,80,256]{2,1,0:T(8,128)(2,1)} %all_to_all.5.recv_ref.refs_0_), custom_call_target="tpu_custom_call" | custom-call | tf_op jit(solution)/shard_map/lead/pallas_call | solution.py:165
  21.5 1.6 %collective-permute-start = (bf16[128,256]{1,0:T(8,128)(2,1)}, bf16[128,256]{1,0:T(8,128)(2,1)S(1)}, u32[]{:S(2)}, u32[]{:S(2)}) collective-permute-start(bf16[128,256]{1,0:T(8,128)(2,1)} %get-tuple-element.11), channel_id=1, source_target_pairs={{0,1},{1,0},{2,3},{3,2},{4,5},{5,4},{6,7},{7,6},{8,9},{9,8},{10,11... | collective-permute-start | bytes 196616 | tf_op jit(solution)/shard_map/ppermute | solution.py:376
  23.1 2.9 %collective-permute-done = bf16[128,256]{1,0:T(8,128)(2,1)S(1)} collective-permute-done((bf16[128,256]{1,0:T(8,128)(2,1)}, bf16[128,256]{1,0:T(8,128)(2,1)S(1)}, u32[]{:S(2)}, u32[]{:S(2)}) %collective-permute-start) | collective-permute-done | bytes 65568 | tf_op jit(solution)/shard_map/ppermute | solution.py:376
  26.0 0.9 add.37
  26.8 2.7 %collective-permute-start.1 = (bf16[128,256]{1,0:T(8,128)(2,1)S(1)}, bf16[128,256]{1,0:T(8,128)(2,1)S(1)}, u32[]{:S(2)}, u32[]{:S(2)}) collective-permute-start(bf16[128,256]{1,0:T(8,128)(2,1)S(1)} %add.37), channel_id=1, source_target_pairs={{0,2},{1,3},{2,0},{3,1},{4,6},{5,7},{6,4},{7,5},{8,10},{9,11},{10,... | collective-permute-start | bytes 196616 | tf_op jit(solution)/shard_map/ppermute | solution.py:376
  29.5 0.1 pad_add_fusion.place_ref
  29.6 2.5 %collective-permute-done.1 = bf16[128,256]{1,0:T(8,128)(2,1)S(1)} collective-permute-done((bf16[128,256]{1,0:T(8,128)(2,1)S(1)}, bf16[128,256]{1,0:T(8,128)(2,1)S(1)}, u32[]{:S(2)}, u32[]{:S(2)}) %collective-permute-start.1) | collective-permute-done | bytes 65568 | tf_op jit(solution)/shard_map/ppermute | solution.py:376
  32.1 4.2 %collective-permute-start.4 = (bf16[128,256]{1,0:T(8,128)(2,1)}, bf16[128,256]{1,0:T(8,128)(2,1)S(1)}, u32[]{:S(2)}, u32[]{:S(2)}) collective-permute-start(bf16[128,256]{1,0:T(8,128)(2,1)} %get-tuple-element.14), channel_id=1, source_target_pairs={{0,3},{1,0},{2,1},{3,2},{4,7},{5,4},{6,5},{7,6},{8,11},{9,8},{10,9... | collective-permute-start | bytes 196616 | tf_op jit(solution)/shard_map/ppermute | solution.py:372
  36.3 0.0 collective-permute-start.3
  36.3 0.6 collective-permute-start.2
  37.0 8.9 %all_gather.3.cols_ref.refs_6_ = bf16[1024,256]{1,0:T(8,128)(2,1)S(1)} all-gather(bf16[128,256]{1,0:T(8,128)(2,1)S(1)} %add.38), channel_id=1, replica_groups=mesh['row'=8,'col'=4] {'row'}, dimensions={0}, use_global_device_ids=true | all-gather | bytes 589824 | tf_op jit(solution)/shard_map/all_gather | solution.py:416
  45.9 0.0 collective-permute-done.4
  45.9 0.0 collective-permute-done.3
  45.9 0.0 collective-permute-done.2
  45.9 0.9 add_add_fusion
  46.7 0.0 copy-start
  46.7 1.5 %collective-permute-start.9 = (bf16[128,256]{1,0:T(8,128)(2,1)S(1)}, bf16[128,256]{1,0:T(8,128)(2,1)S(1)}, u32[]{:S(2)}, u32[]{:S(2)}) collective-permute-start(bf16[128,256]{1,0:T(8,128)(2,1)S(1)} %add_add_fusion), channel_id=1, source_target_pairs={{16,0},{20,1},{24,2},{28,3},{17,4},{21,5},{25,6},{29,7},{18,8},{22... | collective-permute-start | bytes 196616 | tf_op jit(solution)/shard_map/ppermute | solution.py:397
  48.3 0.7 collective-permute-start.8
  48.9 8.4 %collective-permute-start.7 = (bf16[8,80,256]{2,1,0:T(8,128)(2,1)}, bf16[8,80,256]{2,1,0:T(8,128)(2,1)S(1)}, u32[]{:S(2)}, u32[]{:S(2)}) collective-permute-start(bf16[8,80,256]{2,1,0:T(8,128)(2,1)} %all_to_all.5.recv_ref.refs_0_), channel_id=1, source_target_pairs={{0,3},{1,0},{2,1},{3,2},{4,7},{5,4},{6,5},{7,6},{8,11},{9,8},{10,9... | collective-permute-start | bytes 983048 | tf_op jit(solution)/shard_map/ppermute | solution.py:372
  57.3 0.0 collective-permute-start.6
  57.3 0.6 collective-permute-start.5
  57.9 61.6 %cholesky.1.refs_7_ = f32[1024,1024]{1,0:T(8,128)S(1)} custom-call(bf16[1024,256]{1,0:T(8,128)(2,1)S(1)} %all_gather.3.cols_ref.refs_6_), custom_call_target="tpu_custom_call" | custom-call | flops 40000000000 | bytes 5242880 | tf_op jit(solution)/shard_map/cholesky/pallas_call | solution.py:246
  119.5 0.0 collective-permute-done.9.refs_5_
  119.5 0.0 collective-permute-done.8.refs_4_
  119.6 0.0 collective-permute-done.7.refs_3_
  119.6 0.0 collective-permute-done.6.refs_2_
  119.6 0.0 collective-permute-done.5.refs_1_
  119.6 0.0 copy-done
  119.6 22.0 %panels.1 = (f32[4096,128]{1,0:T(8,128)}, f32[4096,128]{1,0:T(8,128)}) custom-call(s32[4]{0:T(128)S(1)} %pad_add_fusion.place_ref, bf16[8,80,256]{2,1,0:T(8,128)(2,1)S(1)} %copy-done, bf16[8,80,256]{2,1,0:T(8,128)(2,1)S(1)} %collective-permute-done.5.refs_1_, bf16[8,80,256]{2,1,0:T(8,128)(2,1)S(1)} %collective-permute-done.6.refs_2_, ...), custom_call_target="tpu_custom_call" | custom-call | tf_op jit(solution)/shard_map/panels/pallas_call | solution.py:348
  (1 shorter events, 0.0 us)
Async XLA Ops:
  21.5 4.5 %collective-permute-start = (bf16[128,256]{1,0:T(8,128)(2,1)}, bf16[128,256]{1,0:T(8,128)(2,1)S(1)}, u32[]{:S(2)}, u32[]{:S(2)}) collective-permute-start(bf16[128,256]{1,0:T(8,128)(2,1)} %get-tuple-element.11), channel_id=1, source_target_pairs={{0,1},{1,0},{2,3},{3,2},{4,5},{5,4},{6,7},{7,6},{8,9},{9,8},{10,11... | collective-permute-start | bytes 196616 | tf_op jit(solution)/shard_map/ppermute | solution.py:376
  26.8 5.2 %collective-permute-start.1 = (bf16[128,256]{1,0:T(8,128)(2,1)S(1)}, bf16[128,256]{1,0:T(8,128)(2,1)S(1)}, u32[]{:S(2)}, u32[]{:S(2)}) collective-permute-start(bf16[128,256]{1,0:T(8,128)(2,1)S(1)} %add.37), channel_id=1, source_target_pairs={{0,2},{1,3},{2,0},{3,1},{4,6},{5,7},{6,4},{7,5},{8,10},{9,11},{10,... | collective-permute-start | bytes 196616 | tf_op jit(solution)/shard_map/ppermute | solution.py:376
  32.1 13.8 %collective-permute-start.4 = (bf16[128,256]{1,0:T(8,128)(2,1)}, bf16[128,256]{1,0:T(8,128)(2,1)S(1)}, u32[]{:S(2)}, u32[]{:S(2)}) collective-permute-start(bf16[128,256]{1,0:T(8,128)(2,1)} %get-tuple-element.14), channel_id=1, source_target_pairs={{0,3},{1,0},{2,1},{3,2},{4,7},{5,4},{6,5},{7,6},{8,11},{9,8},{10,9... | collective-permute-start | bytes 196616 | tf_op jit(solution)/shard_map/ppermute | solution.py:372
  36.3 9.5 %collective-permute-start.3 = (bf16[128,256]{1,0:T(8,128)(2,1)}, bf16[128,256]{1,0:T(8,128)(2,1)S(1)}, u32[]{:S(2)}, u32[]{:S(2)}) collective-permute-start(bf16[128,256]{1,0:T(8,128)(2,1)} %get-tuple-element.14), channel_id=1, source_target_pairs={{0,2},{1,3},{2,0},{3,1},{4,6},{5,7},{6,4},{7,5},{8,10},{9,11},{10,... | collective-permute-start | bytes 196616 | tf_op jit(solution)/shard_map/ppermute | solution.py:372
  36.3 9.5 %collective-permute-start.2 = (bf16[128,256]{1,0:T(8,128)(2,1)}, bf16[128,256]{1,0:T(8,128)(2,1)S(1)}, u32[]{:S(2)}, u32[]{:S(2)}) collective-permute-start(bf16[128,256]{1,0:T(8,128)(2,1)} %get-tuple-element.14), channel_id=1, source_target_pairs={{0,1},{1,2},{2,3},{3,0},{4,5},{5,6},{6,7},{7,4},{8,9},{9,10},{10,1... | collective-permute-start | bytes 196616 | tf_op jit(solution)/shard_map/ppermute | solution.py:372
  46.7 72.9 %copy-start = (bf16[8,80,256]{2,1,0:T(8,128)(2,1)S(1)}, bf16[8,80,256]{2,1,0:T(8,128)(2,1)}, u32[]{:S(2)}) copy-start(bf16[8,80,256]{2,1,0:T(8,128)(2,1)} %all_to_all.5.recv_ref.refs_0_) | copy-start | bytes 983044
  46.7 72.8 %collective-permute-start.9 = (bf16[128,256]{1,0:T(8,128)(2,1)S(1)}, bf16[128,256]{1,0:T(8,128)(2,1)S(1)}, u32[]{:S(2)}, u32[]{:S(2)}) collective-permute-start(bf16[128,256]{1,0:T(8,128)(2,1)S(1)} %add_add_fusion), channel_id=1, source_target_pairs={{16,0},{20,1},{24,2},{28,3},{17,4},{21,5},{25,6},{29,7},{18,8},{22... | collective-permute-start | bytes 196616 | tf_op jit(solution)/shard_map/ppermute | solution.py:397
  48.3 71.3 %collective-permute-start.8 = (bf16[128,256]{1,0:T(8,128)(2,1)S(1)}, bf16[128,256]{1,0:T(8,128)(2,1)S(1)}, u32[]{:S(2)}, u32[]{:S(2)}) collective-permute-start(bf16[128,256]{1,0:T(8,128)(2,1)S(1)} %add_add_fusion), channel_id=1, source_target_pairs={{0,0},{4,1},{8,2},{12,3},{1,4},{5,5},{9,6},{13,7},{2,8},{6,9},{10,... | collective-permute-start | bytes 196616 | tf_op jit(solution)/shard_map/ppermute | solution.py:397
  48.9 70.6 %collective-permute-start.7 = (bf16[8,80,256]{2,1,0:T(8,128)(2,1)}, bf16[8,80,256]{2,1,0:T(8,128)(2,1)S(1)}, u32[]{:S(2)}, u32[]{:S(2)}) collective-permute-start(bf16[8,80,256]{2,1,0:T(8,128)(2,1)} %all_to_all.5.recv_ref.refs_0_), channel_id=1, source_target_pairs={{0,3},{1,0},{2,1},{3,2},{4,7},{5,4},{6,5},{7,6},{8,11},{9,8},{10,9... | collective-permute-start | bytes 983048 | tf_op jit(solution)/shard_map/ppermute | solution.py:372
  57.3 62.3 %collective-permute-start.6 = (bf16[8,80,256]{2,1,0:T(8,128)(2,1)}, bf16[8,80,256]{2,1,0:T(8,128)(2,1)S(1)}, u32[]{:S(2)}, u32[]{:S(2)}) collective-permute-start(bf16[8,80,256]{2,1,0:T(8,128)(2,1)} %all_to_all.5.recv_ref.refs_0_), channel_id=1, source_target_pairs={{0,2},{1,3},{2,0},{3,1},{4,6},{5,7},{6,4},{7,5},{8,10},{9,11},{10,... | collective-permute-start | bytes 983048 | tf_op jit(solution)/shard_map/ppermute | solution.py:372
  57.3 62.3 %collective-permute-start.5 = (bf16[8,80,256]{2,1,0:T(8,128)(2,1)}, bf16[8,80,256]{2,1,0:T(8,128)(2,1)S(1)}, u32[]{:S(2)}, u32[]{:S(2)}) collective-permute-start(bf16[8,80,256]{2,1,0:T(8,128)(2,1)} %all_to_all.5.recv_ref.refs_0_), channel_id=1, source_target_pairs={{0,1},{1,2},{2,3},{3,0},{4,5},{5,6},{6,7},{7,4},{8,9},{9,10},{10,1... | collective-permute-start | bytes 983048 | tf_op jit(solution)/shard_map/ppermute | solution.py:372

commit v3 on v2

--- a/solution.py
+++ b/solution.py
@@ -168,40 +168,54 @@
 
 
 def diag_inverse(block):
-    size, width = block.shape[0], 8
+    size, width, ahead = block.shape[0], 8, 2
     count = size // width
-    sub = iota((width, size), 0)
-    lane = iota((width, size), 1)
+    shape = (width, size)
+    sub, lane = iota(shape, 0), iota(shape, 1)
+    spread = lambda x: jnp.broadcast_to(x, shape)
     left = [block[q * width : (q + 1) * width, :] for q in range(count)]
     right = [jnp.where(lane == sub + q * width, 1.0, 0.0).astype(F32) for q in range(count)]
+    columns = {}
     out = []
     for g in range(count):
-        base = g * width
-        pivot_l, pivot_r = left[g], right[g]
-        cols = [
-            jnp.broadcast_to(pivot_l[:, base + k : base + k + 1], (width, size)) for k in range(width)
-        ]
-        diag = jnp.ones((width, size), F32)
+        rows = range(g, min(g + ahead + 1, count))
+        for q in rows:
+            for h in range(g, min(q, g + ahead - 1) + 1):
+                if (q, h) not in columns:
+                    columns[q, h] = [spread(left[q][:, h * width + k : h * width + k + 1]) for k in range(width)]
+        diag = jnp.ones(shape, F32)
         for i in range(width):
-            own = jnp.broadcast_to(cols[i][i : i + 1, :], (width, size))
+            own = spread(columns[g, g][i][i : i + 1, :])
+            inv = 1.0 / own
             diag = jnp.where(sub == i, own, diag)
-            factor = jnp.where(sub > i, cols[i] / own, 0.0)
-            for k in range(i + 1, width):
-                cols[k] = cols[k] - factor * jnp.broadcast_to(cols[k][i : i + 1, :], (width, size))
-            pivot_l = pivot_l - factor * jnp.broadcast_to(pivot_l[i : i + 1, :], (width, size))
-            pivot_r = pivot_r - factor * jnp.broadcast_to(pivot_r[i : i + 1, :], (width, size))
+            source = {q: columns[q, g][i] for q in rows}
+            factor = {q: source[q] * inv for q in rows}
+            factor[g] = jnp.where(sub > i, factor[g], 0.0)
+            for h in range(g, min(g + ahead, count)):
+                for k in range(i + 1 if h == g else 0, width):
+                    value = spread(source[h][k : k + 1, :])
+                    for q in rows:
+                        if q >= h:
+                            columns[q, h][k] = columns[q, h][k] - factor[q] * value
+            pivot_l, pivot_r = spread(left[g][i : i + 1, :]), spread(right[g][i : i + 1, :])
+            for q in rows:
+                left[q] = left[q] - factor[q] * pivot_l
+                right[q] = right[q] - factor[q] * pivot_r
         scale = lax.rsqrt(diag)
-        pivot_l, pivot_r = pivot_l * scale, pivot_r * scale
+        pivot_l, pivot_r = left[g] * scale, right[g] * scale
         out.append(pivot_r)
-        if g + 1 < count:
-            turned = pivot_l.T
-            for q in range(g + 1, count):
-                rest_l, rest_r = left[q], right[q]
-                for i in range(width):
-                    c = jnp.broadcast_to(turned[q * width : (q + 1) * width, i : i + 1], (width, size))
-                    rest_l = rest_l - c * jnp.broadcast_to(pivot_l[i : i + 1, :], (width, size))
-                    rest_r = rest_r - c * jnp.broadcast_to(pivot_r[i : i + 1, :], (width, size))
-                left[q], right[q] = rest_l, rest_r
+        first = g + ahead + 1
+        if first < count:
+            high = [x.astype(BF16).astype(F32) for x in (pivot_l, pivot_r)]
+            low = [x - h for x, h in zip((pivot_l, pivot_r), high)]
+            zero = jnp.zeros_like(pivot_l)
+            lhs = jnp.concatenate([high[0], high[0], low[0], zero], axis=0).astype(BF16)
+            high, low = jnp.concatenate(high, axis=1), jnp.concatenate(low, axis=1)
+            rhs = jnp.concatenate([high, low, high, jnp.zeros_like(high)], axis=0).astype(BF16)
+            gone = dot(lhs, rhs, TN)
+            for q in range(first, count):
+                left[q] = left[q] - gone[q * width : (q + 1) * width, :size]
+                right[q] = right[q] - gone[q * width : (q + 1) * width, size:]
     return jnp.concatenate(out, axis=0)
 
 
@@ -229,14 +243,15 @@
         high_ref[...] = high
         low_ref[...] = low
 
-        def trail(i, inner):
-            start = pl.multiple_of(i * TILE, TILE)
-            work_ref[pl.ds(start, TILE), pl.ds(base, TILE)] = jnp.zeros((TILE, TILE), F32)
-            lower = (high_ref[:, pl.ds(start, TILE)], low_ref[:, pl.ds(start, TILE)])
-            work_ref[pl.ds(start, TILE), :] -= dot_split(lower, (high_ref[...], low_ref[...]), TN)
-            return inner
-
-        lax.fori_loop(k + 1, blocks, trail, 0)
+        for done in range(1, blocks):
+
+            @pl.when(k == done - 1)
+            def _():
+                rest = slice(done * TILE, PANEL)
+                work_ref[rest, (done - 1) * TILE : done * TILE] = jnp.zeros((PANEL - done * TILE, TILE), F32)
+                lower = (high_ref[:, rest], low_ref[:, rest])
+                work_ref[rest, :] -= dot_split(lower, (high_ref[...], low_ref[...]), TN)
+
         return carry
 
     lax.fori_loop(0, blocks, step, 0)

time: 142 us -> 114 us (0.80)
  Pallas kernels: 91.7 us -> 63.3 us
    pallas_call x1, Pallas kernels: 61.6 us -> 33 us  [make_inverse(): pl.pallas_call(chol_kernel, out_shape=jax.ShapeDtypeStruct((PANEL, PANEL)...]
  transfers between devices with their start and end apart: 10 -> 10, of which waited for: 2 -> 2; matrix products, arithmetic and copies ran while one was open for 0% -> 0% of each run, Pallas kernels for 43% -> 29%
where the time goes in v3:
time: 114 us; the launch traced here: 113 us
  Pallas kernels  63.3 us (56%)
  blocking collectives  21.6 us (19%)
  starting transfers between devices  20.3 us (18%)
  waiting for transfers between devices  5.42 us (5%)
  other arithmetic  1.81 us (2%)
    pallas_call x1, Pallas kernels, make_inverse(): pl.pallas_call(chol_kernel, out_shape=jax.ShapeDtypeStruct((PANEL, PANEL)...  33 us
    pallas_call x1, Pallas kernels, make_outputs(): pl.pallas_call(functools.partial(panel_kernel, share, row_count, col_coun...  22.2 us
    ppermute x6, starting transfers between devices, shift(): lax.ppermute(value, axis, [(i, (i + distance) % size) for i in range(size)])  13.9 us
    all_to_all x1, blocking collectives, per_device(): lax.all_to_all(bucket, 'row', split_axis=0, concat_axis=0, tiled=True)  12.7 us
    all_gather x1, blocking collectives, per_device(): columns = lax.all_gather(first, 'row', axis=0, tiled=True)  8.9 us
    pallas_call x1, Pallas kernels, make_features(): pl.pallas_call(functools.partial(feature_kernel, share, row_count), out_s...  6.28 us
    ppermute x2, waiting for transfers between devices, exchange(): return lax.ppermute(value, axis, [(i, i ^ step) for i in range(size)])  5.4 us
    ppermute x2, starting transfers between devices, exchange(): return lax.ppermute(value, axis, [(i, i ^ step) for i in range(size)])  4.23 us
  transfers between devices with their start and end apart: 10, of which 2 were waited for; matrix products, arithmetic and copies ran while one was open for 0% of the time, Pallas kernels for 29%

profile of v3, /device:TPU:0, one launch (start us, length us, event | category | flops | bytes accessed | tf_op | source)
XLA Modules:
  0.0 113.2 jit_solution(17875357450983237181)
XLA Ops:
  0.6 6.3 %features.1 = bf16[8,80,256]{2,1,0:T(8,128)(2,1)S(1)} custom-call(s32[1,512]{1,0:T(1,128)} %bitcast.10, bf16[512,768]{1,0:T(8,128)(2,1)} %img_ref.1, bf16[768,2048]{1,0:T(8,128)(2,1)} %win_ref.1, f32[1,2048]{1,0:T(1,128)} %bitcast.9, bf16[2048,256]{1,0:T(8,128)(2,1)} %wout_ref.1, f32[1,256]{1,0:T(1,128)} %bitcast.11), custom_call_target="tpu_custom_call" | custom-call | tf_op jit(solution)/shard_map/features/pallas_call | solution.py:115
  6.9 12.7 %all_to_all.5.recv_ref.refs_0_ = bf16[8,80,256]{2,1,0:T(8,128)(2,1)} all-to-all(bf16[8,80,256]{2,1,0:T(8,128)(2,1)S(1)} %features.1), channel_id=1, replica_groups=mesh['row'=8,'col'=4] {'row'}, dimensions={0} | all-to-all | bytes 655360 | tf_op jit(solution)/shard_map/all_to_all | solution.py:427
  19.6 1.8 %lead.1 = (bf16[128,256]{1,0:T(8,128)(2,1)}, bf16[128,256]{1,0:T(8,128)(2,1)}) custom-call(bf16[8,80,256]{2,1,0:T(8,128)(2,1)} %all_to_all.5.recv_ref.refs_0_), custom_call_target="tpu_custom_call" | custom-call | tf_op jit(solution)/shard_map/lead/pallas_call | solution.py:165
  21.5 1.6 %collective-permute-start = (bf16[128,256]{1,0:T(8,128)(2,1)}, bf16[128,256]{1,0:T(8,128)(2,1)S(1)}, u32[]{:S(2)}, u32[]{:S(2)}) collective-permute-start(bf16[128,256]{1,0:T(8,128)(2,1)} %get-tuple-element.11), channel_id=1, source_target_pairs={{0,1},{1,0},{2,3},{3,2},{4,5},{5,4},{6,7},{7,6},{8,9},{9,8},{10,11... | collective-permute-start | bytes 196616 | tf_op jit(solution)/shard_map/ppermute | solution.py:391
  23.1 2.9 %collective-permute-done = bf16[128,256]{1,0:T(8,128)(2,1)S(1)} collective-permute-done((bf16[128,256]{1,0:T(8,128)(2,1)}, bf16[128,256]{1,0:T(8,128)(2,1)S(1)}, u32[]{:S(2)}, u32[]{:S(2)}) %collective-permute-start) | collective-permute-done | bytes 65568 | tf_op jit(solution)/shard_map/ppermute | solution.py:391
  26.0 0.9 add.37
  26.8 2.7 %collective-permute-start.1 = (bf16[128,256]{1,0:T(8,128)(2,1)S(1)}, bf16[128,256]{1,0:T(8,128)(2,1)S(1)}, u32[]{:S(2)}, u32[]{:S(2)}) collective-permute-start(bf16[128,256]{1,0:T(8,128)(2,1)S(1)} %add.37), channel_id=1, source_target_pairs={{0,2},{1,3},{2,0},{3,1},{4,6},{5,7},{6,4},{7,5},{8,10},{9,11},{10,... | collective-permute-start | bytes 196616 | tf_op jit(solution)/shard_map/ppermute | solution.py:391
  29.5 0.1 pad_add_fusion.place_ref
  29.6 2.5 %collective-permute-done.1 = bf16[128,256]{1,0:T(8,128)(2,1)S(1)} collective-permute-done((bf16[128,256]{1,0:T(8,128)(2,1)S(1)}, bf16[128,256]{1,0:T(8,128)(2,1)S(1)}, u32[]{:S(2)}, u32[]{:S(2)}) %collective-permute-start.1) | collective-permute-done | bytes 65568 | tf_op jit(solution)/shard_map/ppermute | solution.py:391
  32.1 4.2 %collective-permute-start.4 = (bf16[128,256]{1,0:T(8,128)(2,1)}, bf16[128,256]{1,0:T(8,128)(2,1)S(1)}, u32[]{:S(2)}, u32[]{:S(2)}) collective-permute-start(bf16[128,256]{1,0:T(8,128)(2,1)} %get-tuple-element.14), channel_id=1, source_target_pairs={{0,3},{1,0},{2,1},{3,2},{4,7},{5,4},{6,5},{7,6},{8,11},{9,8},{10,9... | collective-permute-start | bytes 196616 | tf_op jit(solution)/shard_map/ppermute | solution.py:387
  36.3 0.0 collective-permute-start.3
  36.3 0.6 collective-permute-start.2
  37.0 8.9 %all_gather.3.cols_ref.refs_6_ = bf16[1024,256]{1,0:T(8,128)(2,1)S(1)} all-gather(bf16[128,256]{1,0:T(8,128)(2,1)S(1)} %add.38), channel_id=1, replica_groups=mesh['row'=8,'col'=4] {'row'}, dimensions={0}, use_global_device_ids=true | all-gather | bytes 589824 | tf_op jit(solution)/shard_map/all_gather | solution.py:431
  45.9 0.0 collective-permute-done.4
  45.9 0.0 collective-permute-done.3
  45.9 0.0 collective-permute-done.2
  45.9 0.9 add_add_fusion
  46.7 0.0 copy-start
  46.7 1.5 %collective-permute-start.9 = (bf16[128,256]{1,0:T(8,128)(2,1)S(1)}, bf16[128,256]{1,0:T(8,128)(2,1)S(1)}, u32[]{:S(2)}, u32[]{:S(2)}) collective-permute-start(bf16[128,256]{1,0:T(8,128)(2,1)S(1)} %add_add_fusion), channel_id=1, source_target_pairs={{16,0},{20,1},{24,2},{28,3},{17,4},{21,5},{25,6},{29,7},{18,8},{22... | collective-permute-start | bytes 196616 | tf_op jit(solution)/shard_map/ppermute | solution.py:412
  48.3 0.7 collective-permute-start.8
  48.9 8.4 %collective-permute-start.7 = (bf16[8,80,256]{2,1,0:T(8,128)(2,1)}, bf16[8,80,256]{2,1,0:T(8,128)(2,1)S(1)}, u32[]{:S(2)}, u32[]{:S(2)}) collective-permute-start(bf16[8,80,256]{2,1,0:T(8,128)(2,1)} %all_to_all.5.recv_ref.refs_0_), channel_id=1, source_target_pairs={{0,3},{1,0},{2,1},{3,2},{4,7},{5,4},{6,5},{7,6},{8,11},{9,8},{10,9... | collective-permute-start | bytes 983048 | tf_op jit(solution)/shard_map/ppermute | solution.py:387
  57.3 0.0 collective-permute-start.6
  57.3 0.6 collective-permute-start.5
  57.9 33.0 %cholesky.1.refs_7_ = f32[1024,1024]{1,0:T(8,128)S(1)} custom-call(bf16[1024,256]{1,0:T(8,128)(2,1)S(1)} %all_gather.3.cols_ref.refs_6_), custom_call_target="tpu_custom_call" | custom-call | flops 40000000000 | bytes 5242880 | tf_op jit(solution)/shard_map/cholesky/pallas_call | solution.py:261
  90.9 0.0 collective-permute-done.9.refs_5_
  90.9 0.0 collective-permute-done.8.refs_4_
  90.9 0.0 collective-permute-done.7.refs_3_
  90.9 0.0 collective-permute-done.6.refs_2_
  91.0 0.0 collective-permute-done.5.refs_1_
  91.0 0.0 copy-done
  91.0 22.2 %panels.1 = (f32[4096,128]{1,0:T(8,128)}, f32[4096,128]{1,0:T(8,128)}) custom-call(s32[4]{0:T(128)S(1)} %pad_add_fusion.place_ref, bf16[8,80,256]{2,1,0:T(8,128)(2,1)S(1)} %copy-done, bf16[8,80,256]{2,1,0:T(8,128)(2,1)S(1)} %collective-permute-done.5.refs_1_, bf16[8,80,256]{2,1,0:T(8,128)(2,1)S(1)} %collective-permute-done.6.refs_2_, ...), custom_call_target="tpu_custom_call" | custom-call | tf_op jit(solution)/shard_map/panels/pallas_call | solution.py:363
  (1 shorter events, 0.0 us)
Async XLA Ops:
  21.5 4.5 %collective-permute-start = (bf16[128,256]{1,0:T(8,128)(2,1)}, bf16[128,256]{1,0:T(8,128)(2,1)S(1)}, u32[]{:S(2)}, u32[]{:S(2)}) collective-permute-start(bf16[128,256]{1,0:T(8,128)(2,1)} %get-tuple-element.11), channel_id=1, source_target_pairs={{0,1},{1,0},{2,3},{3,2},{4,5},{5,4},{6,7},{7,6},{8,9},{9,8},{10,11... | collective-permute-start | bytes 196616 | tf_op jit(solution)/shard_map/ppermute | solution.py:391
  26.8 5.2 %collective-permute-start.1 = (bf16[128,256]{1,0:T(8,128)(2,1)S(1)}, bf16[128,256]{1,0:T(8,128)(2,1)S(1)}, u32[]{:S(2)}, u32[]{:S(2)}) collective-permute-start(bf16[128,256]{1,0:T(8,128)(2,1)S(1)} %add.37), channel_id=1, source_target_pairs={{0,2},{1,3},{2,0},{3,1},{4,6},{5,7},{6,4},{7,5},{8,10},{9,11},{10,... | collective-permute-start | bytes 196616 | tf_op jit(solution)/shard_map/ppermute | solution.py:391
  32.1 13.8 %collective-permute-start.4 = (bf16[128,256]{1,0:T(8,128)(2,1)}, bf16[128,256]{1,0:T(8,128)(2,1)S(1)}, u32[]{:S(2)}, u32[]{:S(2)}) collective-permute-start(bf16[128,256]{1,0:T(8,128)(2,1)} %get-tuple-element.14), channel_id=1, source_target_pairs={{0,3},{1,0},{2,1},{3,2},{4,7},{5,4},{6,5},{7,6},{8,11},{9,8},{10,9... | collective-permute-start | bytes 196616 | tf_op jit(solution)/shard_map/ppermute | solution.py:387
  36.3 9.5 %collective-permute-start.3 = (bf16[128,256]{1,0:T(8,128)(2,1)}, bf16[128,256]{1,0:T(8,128)(2,1)S(1)}, u32[]{:S(2)}, u32[]{:S(2)}) collective-permute-start(bf16[128,256]{1,0:T(8,128)(2,1)} %get-tuple-element.14), channel_id=1, source_target_pairs={{0,2},{1,3},{2,0},{3,1},{4,6},{5,7},{6,4},{7,5},{8,10},{9,11},{10,... | collective-permute-start | bytes 196616 | tf_op jit(solution)/shard_map/ppermute | solution.py:387
  36.3 9.5 %collective-permute-start.2 = (bf16[128,256]{1,0:T(8,128)(2,1)}, bf16[128,256]{1,0:T(8,128)(2,1)S(1)}, u32[]{:S(2)}, u32[]{:S(2)}) collective-permute-start(bf16[128,256]{1,0:T(8,128)(2,1)} %get-tuple-element.14), channel_id=1, source_target_pairs={{0,1},{1,2},{2,3},{3,0},{4,5},{5,6},{6,7},{7,4},{8,9},{9,10},{10,1... | collective-permute-start | bytes 196616 | tf_op jit(solution)/shard_map/ppermute | solution.py:387
  46.7 44.2 %copy-start = (bf16[8,80,256]{2,1,0:T(8,128)(2,1)S(1)}, bf16[8,80,256]{2,1,0:T(8,128)(2,1)}, u32[]{:S(2)}) copy-start(bf16[8,80,256]{2,1,0:T(8,128)(2,1)} %all_to_all.5.recv_ref.refs_0_) | copy-start | bytes 983044
  46.7 44.2 %collective-permute-start.9 = (bf16[128,256]{1,0:T(8,128)(2,1)S(1)}, bf16[128,256]{1,0:T(8,128)(2,1)S(1)}, u32[]{:S(2)}, u32[]{:S(2)}) collective-permute-start(bf16[128,256]{1,0:T(8,128)(2,1)S(1)} %add_add_fusion), channel_id=1, source_target_pairs={{16,0},{20,1},{24,2},{28,3},{17,4},{21,5},{25,6},{29,7},{18,8},{22... | collective-permute-start | bytes 196616 | tf_op jit(solution)/shard_map/ppermute | solution.py:412
  48.3 42.7 %collective-permute-start.8 = (bf16[128,256]{1,0:T(8,128)(2,1)S(1)}, bf16[128,256]{1,0:T(8,128)(2,1)S(1)}, u32[]{:S(2)}, u32[]{:S(2)}) collective-permute-start(bf16[128,256]{1,0:T(8,128)(2,1)S(1)} %add_add_fusion), channel_id=1, source_target_pairs={{0,0},{4,1},{8,2},{12,3},{1,4},{5,5},{9,6},{13,7},{2,8},{6,9},{10,... | collective-permute-start | bytes 196616 | tf_op jit(solution)/shard_map/ppermute | solution.py:412
  48.9 42.0 %collective-permute-start.7 = (bf16[8,80,256]{2,1,0:T(8,128)(2,1)}, bf16[8,80,256]{2,1,0:T(8,128)(2,1)S(1)}, u32[]{:S(2)}, u32[]{:S(2)}) collective-permute-start(bf16[8,80,256]{2,1,0:T(8,128)(2,1)} %all_to_all.5.recv_ref.refs_0_), channel_id=1, source_target_pairs={{0,3},{1,0},{2,1},{3,2},{4,7},{5,4},{6,5},{7,6},{8,11},{9,8},{10,9... | collective-permute-start | bytes 983048 | tf_op jit(solution)/shard_map/ppermute | solution.py:387
  57.3 33.7 %collective-permute-start.6 = (bf16[8,80,256]{2,1,0:T(8,128)(2,1)}, bf16[8,80,256]{2,1,0:T(8,128)(2,1)S(1)}, u32[]{:S(2)}, u32[]{:S(2)}) collective-permute-start(bf16[8,80,256]{2,1,0:T(8,128)(2,1)} %all_to_all.5.recv_ref.refs_0_), channel_id=1, source_target_pairs={{0,2},{1,3},{2,0},{3,1},{4,6},{5,7},{6,4},{7,5},{8,10},{9,11},{10,... | collective-permute-start | bytes 983048 | tf_op jit(solution)/shard_map/ppermute | solution.py:387
  57.3 33.7 %collective-permute-start.5 = (bf16[8,80,256]{2,1,0:T(8,128)(2,1)}, bf16[8,80,256]{2,1,0:T(8,128)(2,1)S(1)}, u32[]{:S(2)}, u32[]{:S(2)}) collective-permute-start(bf16[8,80,256]{2,1,0:T(8,128)(2,1)} %all_to_all.5.recv_ref.refs_0_), channel_id=1, source_target_pairs={{0,1},{1,2},{2,3},{3,0},{4,5},{5,6},{6,7},{7,4},{8,9},{9,10},{10,1... | collective-permute-start | bytes 983048 | tf_op jit(solution)/shard_map/ppermute | solution.py:387

commit v4 on v3

--- a/solution.py
+++ b/solution.py
@@ -103,7 +103,7 @@
     rows, din = images.shape
     hid, feat = weight_out.shape
     share = rows // row_count
-    block = 512
+    block = 1024
     operands = (
         position.reshape(1, rows),
         images,
@@ -148,22 +148,20 @@
     )
 
 
-def lead_kernel(share, recv_ref, *out_refs):
+def lead_kernel(share, recv_ref, out_ref):
     groups = recv_ref.shape[0] * share // TILE
     slots = [read_slots(recv_ref, (), share, g) for g in range(groups)]
     rows = jnp.concatenate([gather_rows(recv_ref, (), share, g) for g in range(groups)], axis=0)
-    for t, out_ref in enumerate(out_refs):
-        pick = jnp.concatenate(
-            [one_hot(iota((TILE, TILE), 0) + t * TILE == s) for s in slots], axis=1
-        )
-        out_ref[...] = dot(pick, rows).astype(BF16)
+    shape = (out_ref.shape[0], TILE)
+    pick = jnp.concatenate([one_hot(iota(shape, 0) == s) for s in slots], axis=1)
+    out_ref[...] = dot(pick, rows).astype(BF16)
 
 
 def make_lead(received, share, lead_tiles):
-    feat = received.shape[2]
-    shape = jax.ShapeDtypeStruct((TILE, feat), BF16)
     return pl.pallas_call(
-        functools.partial(lead_kernel, share), out_shape=[shape] * lead_tiles, name="lead"
+        functools.partial(lead_kernel, share),
+        out_shape=jax.ShapeDtypeStruct((lead_tiles * TILE, received.shape[2]), BF16),
+        name="lead",
     )(received)
 
 
@@ -274,7 +272,7 @@
 
 def panel_kernel(share, row_count, col_count, rows_blk, parts, pieces, place_ref, *refs):
     recv_refs, next_refs = refs[:parts], refs[parts : parts + pieces]
-    (cols_ref, inv_ref, panel_ref, update_ref, feats_ref, slots_ref, high_ref, low_ref, half_ref,
+    (cols_ref, inv_ref, panel_ref, update_ref, feats_ref, slots_ref, high_ref, half_ref,
      own_ref, own_half_ref) = refs[parts + pieces :]
     step = pl.program_id(0)
     row_index, col_index = place_ref[0], place_ref[1]
@@ -312,8 +310,9 @@
         solved = dot_split(split(dot_split(split(cross), inverse, NT)), inverse)
         right = jnp.concatenate(own + [solved], axis=0)
         high, low = split(right.T)
-        high_ref[...] = high
-        low_ref[...] = low
+        high_ref[0:PANEL, :] = high
+        high_ref[PANEL : 2 * PANEL, :] = low
+        high_ref[2 * PANEL :, :] = high
 
     def body(diagonal):
         slot = iota((rows_blk, TILE), 0) + step * rows_blk
@@ -331,7 +330,8 @@
             index = iota((rows_blk, width), 1)
             column = PANEL + (index // TILE * col_count + col_index) * TILE + index % TILE
             kern_next = kern_next + jnp.where(place == column, noise_var, 0.0)
-        result = dot_split(split(kern), (high_ref[...], low_ref[...]))
+        high, low = split(kern)
+        result = dot(jnp.concatenate([high, high, low], axis=1), high_ref[...])
         update = kern_next - result[:, width:]
         for t in range(col_tiles):
             where = pl.ds(t, rows_blk, stride=col_tiles) if col_tiles > 1 else slice(None)
@@ -355,7 +355,7 @@
     local_rows = len(parts) * parts[0].shape[0] * share
     col_tiles = PANEL // TILE // col_count
     width = col_tiles * TILE
-    rows_blk = 256
+    rows_blk = 512
     place = jnp.stack([lax.axis_index("row"), lax.axis_index("col")] + piece_tiles).astype(jnp.int32)
     operands = (*parts, *pieces, columns, inverse)
     out = jax.ShapeDtypeStruct((local_rows * col_tiles, TILE), F32)
@@ -371,8 +371,7 @@
             scratch_shapes=[
                 pltpu.VMEM((local_rows, feat), BF16),
                 pltpu.VMEM((8, local_rows), jnp.int32),
-                pltpu.VMEM((PANEL, 2 * width), BF16),
-                pltpu.VMEM((PANEL, 2 * width), BF16),
+                pltpu.VMEM((3 * PANEL, 2 * width), BF16),
                 pltpu.VMEM((8, PANEL), F32),
                 pltpu.VMEM((width, feat), BF16),
                 pltpu.VMEM((8, width), F32),
@@ -426,17 +425,15 @@
     )
     received = lax.all_to_all(bucket, "row", split_axis=0, concat_axis=0, tiled=True)
     lead = make_lead(received, share, lead_tiles)
-    first, rest = lax.optimization_barrier((sum_over(lead[0], "col", col_count), lead[1:]))
-    rest = [[tile] + [shift(tile, "col", d, col_count) for d in range(1, col_count)] for tile in rest]
-    columns = lax.all_gather(first, "row", axis=0, tiled=True)
-    rest = [sum(pieces[1:], pieces[0]) for pieces in rest]
-    columns, rest, received = lax.optimization_barrier((columns, rest, received))
-    if rest:
-        pieces, piece_tiles = next_tiles(rest[0], row_count, col_count)
-    else:
+    lead = sum_over(lead, "col", col_count)
+    lead, received = lax.optimization_barrier((lead, received))
+    parts = [received] + [shift(received, "col", d, col_count) for d in range(1, col_count)]
+    if lead_tiles > 1:
+        pieces, piece_tiles = next_tiles(lead[TILE : 2 * TILE], row_count, col_count)
+    columns = lax.all_gather(lead[:TILE], "row", axis=0, tiled=True)
+    if lead_tiles == 1:
         pieces = [columns[PANEL + t * TILE : PANEL + (t + 1) * TILE] for t in range(PANEL // TILE)]
         piece_tiles = [jnp.int32(t) for t in range(PANEL // TILE)]
-    parts = [received] + [shift(received, "col", d, col_count) for d in range(1, col_count)]
     inverse = make_inverse(columns[:PANEL])
     panel, update = make_outputs(
         parts, pieces, piece_tiles, columns[:PANEL], inverse, share, row_count, col_count

time: 114 us -> 110 us (0.965)
  the two profiles are of different devices: /device:TPU:0 before, /device:TPU:11 now
where the time goes in v4:
time: 110 us; the launch traced here: 109 us
  Pallas kernels  61 us (55%)
  blocking collectives  24.7 us (22%)
  starting transfers between devices  11.6 us (11%)
  waiting for transfers between devices  9.94 us (9%)
    pallas_call x1, Pallas kernels, make_inverse(): pl.pallas_call(chol_kernel, out_shape=jax.ShapeDtypeStruct((PANEL, PANEL)...  33 us
    pallas_call x1, Pallas kernels, make_outputs(): pl.pallas_call(functools.partial(panel_kernel, share, row_count, col_coun...  20.6 us
    all_gather x1, blocking collectives, per_device(): columns = lax.all_gather(lead[:TILE], 'row', axis=0, tiled=True)  14.2 us
    all_to_all x1, blocking collectives, per_device(): lax.all_to_all(bucket, 'row', split_axis=0, concat_axis=0, tiled=True)  10.5 us
    ppermute x2, waiting for transfers between devices, exchange(): return lax.ppermute(value, axis, [(i, i ^ step) for i in range(size)])  9.93 us
    ppermute x2, starting transfers between devices, next_tiles(): pieces.append(lax.ppermute(tile, ('row', 'col'), pairs))  5.58 us
    pallas_call x1, Pallas kernels, make_features(): pl.pallas_call(functools.partial(feature_kernel, share, row_count), out_s...  5.55 us
    ppermute x3, starting transfers between devices, shift(): lax.ppermute(value, axis, [(i, (i + distance) % size) for i in range(size)])  3.53 us
  transfers between devices with their start and end apart: 7, of which 2 were waited for; matrix products, arithmetic and copies ran while one was open for 0% of the time, Pallas kernels for 30%

profile of v4, /device:TPU:11, one launch (start us, length us, event | category | flops | bytes accessed | tf_op | source)
XLA Modules:
  0.0 109.0 jit_solution(3219268096012218417)
XLA Ops:
  0.6 5.6 %features.1 = bf16[8,80,256]{2,1,0:T(8,128)(2,1)S(1)} custom-call(s32[1,512]{1,0:T(1,128)} %bitcast.10, bf16[512,768]{1,0:T(8,128)(2,1)} %img_ref.1, bf16[768,2048]{1,0:T(8,128)(2,1)} %win_ref.1, f32[1,2048]{1,0:T(1,128)} %bitcast.9, bf16[2048,256]{1,0:T(8,128)(2,1)} %wout_ref.1, f32[1,256]{1,0:T(1,128)} %bitcast.11), custom_call_target="tpu_custom_call" | custom-call | tf_op jit(solution)/shard_map/features/pallas_call | solution.py:115
  6.2 10.5 %all_to_all.5.recv_ref.refs_0_ = bf16[8,80,256]{2,1,0:T(8,128)(2,1)} all-to-all(bf16[8,80,256]{2,1,0:T(8,128)(2,1)S(1)} %features.1), channel_id=1, replica_groups=mesh['row'=8,'col'=4] {'row'}, dimensions={0} | all-to-all | bytes 655360 | tf_op jit(solution)/shard_map/all_to_all | solution.py:426
  16.6 1.9 %lead.1 = bf16[256,256]{1,0:T(8,128)(2,1)} custom-call(bf16[8,80,256]{2,1,0:T(8,128)(2,1)} %all_to_all.5.recv_ref.refs_0_), custom_call_target="tpu_custom_call" | custom-call | tf_op jit(solution)/shard_map/lead/pallas_call | solution.py:161
  18.5 0.2 collective-permute-start
  18.7 4.5 %collective-permute-done = bf16[256,256]{1,0:T(8,128)(2,1)S(1)} collective-permute-done((bf16[256,256]{1,0:T(8,128)(2,1)}, bf16[256,256]{1,0:T(8,128)(2,1)S(1)}, u32[]{:S(2)}, u32[]{:S(2)}) %collective-permute-start) | collective-permute-done | bytes 131104 | tf_op jit(solution)/shard_map/ppermute | solution.py:390
  23.2 0.9 add.28
  24.2 2.4 %collective-permute-start.1 = (bf16[256,256]{1,0:T(8,128)(2,1)S(1)}, bf16[256,256]{1,0:T(8,128)(2,1)S(1)}, u32[]{:S(2)}, u32[]{:S(2)}) collective-permute-start(bf16[256,256]{1,0:T(8,128)(2,1)S(1)} %add.28), channel_id=1, source_target_pairs={{0,2},{1,3},{2,0},{3,1},{4,6},{5,7},{6,4},{7,5},{8,10},{9,11},{10,... | collective-permute-start | bytes 393224 | tf_op jit(solution)/shard_map/ppermute | solution.py:390
  26.5 0.1 pad_add_fusion.place_ref
  26.6 5.4 %collective-permute-done.1 = bf16[256,256]{1,0:T(8,128)(2,1)S(1)} collective-permute-done((bf16[256,256]{1,0:T(8,128)(2,1)S(1)}, bf16[256,256]{1,0:T(8,128)(2,1)S(1)}, u32[]{:S(2)}, u32[]{:S(2)}) %collective-permute-start.1) | collective-permute-done | bytes 131104 | tf_op jit(solution)/shard_map/ppermute | solution.py:390
  32.0 3.7 %collective-permute-start.6 = (bf16[128,256]{1,0:T(8,128)(2,1)S(1)}, bf16[128,256]{1,0:T(8,128)(2,1)S(1)}, u32[]{:S(2)}, u32[]{:S(2)}) collective-permute-start(bf16[128,256]{1,0:T(8,128)(2,1)S(1)} %get-tuple-element.11), channel_id=1, source_target_pairs={{16,0},{20,1},{24,2},{28,3},{17,4},{21,5},{25,6},{29,7},{18,8},{22... | collective-permute-start | bytes 196616 | tf_op jit(solution)/shard_map/ppermute | solution.py:411
  35.7 1.9 %collective-permute-start.5 = (bf16[128,256]{1,0:T(8,128)(2,1)S(1)}, bf16[128,256]{1,0:T(8,128)(2,1)S(1)}, u32[]{:S(2)}, u32[]{:S(2)}) collective-permute-start(bf16[128,256]{1,0:T(8,128)(2,1)S(1)} %get-tuple-element.11), channel_id=1, source_target_pairs={{0,0},{4,1},{8,2},{12,3},{1,4},{5,5},{9,6},{13,7},{2,8},{6,9},{10,... | collective-permute-start | bytes 196616 | tf_op jit(solution)/shard_map/ppermute | solution.py:411
  37.6 2.3 %collective-permute-start.4 = (bf16[8,80,256]{2,1,0:T(8,128)(2,1)}, bf16[8,80,256]{2,1,0:T(8,128)(2,1)S(1)}, u32[]{:S(2)}, u32[]{:S(2)}) collective-permute-start(bf16[8,80,256]{2,1,0:T(8,128)(2,1)} %all_to_all.5.recv_ref.refs_0_), channel_id=1, source_target_pairs={{0,3},{1,0},{2,1},{3,2},{4,7},{5,4},{6,5},{7,6},{8,11},{9,8},{10,9... | collective-permute-start | bytes 983048 | tf_op jit(solution)/shard_map/ppermute | solution.py:386
  39.9 0.0 collective-permute-start.3
  39.9 1.3 %collective-permute-start.2 = (bf16[8,80,256]{2,1,0:T(8,128)(2,1)}, bf16[8,80,256]{2,1,0:T(8,128)(2,1)S(1)}, u32[]{:S(2)}, u32[]{:S(2)}) collective-permute-start(bf16[8,80,256]{2,1,0:T(8,128)(2,1)} %all_to_all.5.recv_ref.refs_0_), channel_id=1, source_target_pairs={{0,1},{1,2},{2,3},{3,0},{4,5},{5,6},{6,7},{7,4},{8,9},{9,10},{10,1... | collective-permute-start | bytes 983048 | tf_op jit(solution)/shard_map/ppermute | solution.py:386
  41.2 14.2 %all_gather.3.cols_ref.refs_6_ = bf16[1024,256]{1,0:T(8,128)(2,1)S(1)} all-gather(bf16[128,256]{1,0:T(8,128)(2,1)S(1)} %get-tuple-element.10), channel_id=1, replica_groups=mesh['row'=8,'col'=4] {'row'}, dimensions={0}, use_global_device_ids=true | all-gather | bytes 589824 | tf_op jit(solution)/shard_map/all_gather | solution.py:433
  55.4 0.0 copy-start
  55.4 33.0 %cholesky.1.refs_7_ = f32[1024,1024]{1,0:T(8,128)S(1)} custom-call(bf16[1024,256]{1,0:T(8,128)(2,1)S(1)} %all_gather.3.cols_ref.refs_6_), custom_call_target="tpu_custom_call" | custom-call | flops 40000000000 | bytes 5242880 | tf_op jit(solution)/shard_map/cholesky/pallas_call | solution.py:259
  88.4 0.0 collective-permute-done.6.refs_5_
  88.4 0.0 collective-permute-done.5.refs_4_
  88.4 0.0 collective-permute-done.4.refs_3_
  88.4 0.0 collective-permute-done.3.refs_2_
  88.4 0.0 collective-permute-done.2.refs_1_
  88.4 0.0 copy-done
  88.4 20.6 %panels.1 = (f32[4096,128]{1,0:T(8,128)}, f32[4096,128]{1,0:T(8,128)}) custom-call(s32[4]{0:T(128)S(1)} %pad_add_fusion.place_ref, bf16[8,80,256]{2,1,0:T(8,128)(2,1)S(1)} %copy-done, bf16[8,80,256]{2,1,0:T(8,128)(2,1)S(1)} %collective-permute-done.2.refs_1_, bf16[8,80,256]{2,1,0:T(8,128)(2,1)S(1)} %collective-permute-done.3.refs_2_, ...), custom_call_target="tpu_custom_call" | custom-call | tf_op jit(solution)/shard_map/panels/pallas_call | solution.py:363
  (2 shorter events, 0.0 us)
Async XLA Ops:
  18.5 4.7 %collective-permute-start = (bf16[256,256]{1,0:T(8,128)(2,1)}, bf16[256,256]{1,0:T(8,128)(2,1)S(1)}, u32[]{:S(2)}, u32[]{:S(2)}) collective-permute-start(bf16[256,256]{1,0:T(8,128)(2,1)} %lead.1), channel_id=1, source_target_pairs={{0,1},{1,0},{2,3},{3,2},{4,5},{5,4},{6,7},{7,6},{8,9},{9,8},{10,11... | collective-permute-start | bytes 393224 | tf_op jit(solution)/shard_map/ppermute | solution.py:390
  24.2 7.8 %collective-permute-start.1 = (bf16[256,256]{1,0:T(8,128)(2,1)S(1)}, bf16[256,256]{1,0:T(8,128)(2,1)S(1)}, u32[]{:S(2)}, u32[]{:S(2)}) collective-permute-start(bf16[256,256]{1,0:T(8,128)(2,1)S(1)} %add.28), channel_id=1, source_target_pairs={{0,2},{1,3},{2,0},{3,1},{4,6},{5,7},{6,4},{7,5},{8,10},{9,11},{10,... | collective-permute-start | bytes 393224 | tf_op jit(solution)/shard_map/ppermute | solution.py:390
  32.0 56.3 %collective-permute-start.6 = (bf16[128,256]{1,0:T(8,128)(2,1)S(1)}, bf16[128,256]{1,0:T(8,128)(2,1)S(1)}, u32[]{:S(2)}, u32[]{:S(2)}) collective-permute-start(bf16[128,256]{1,0:T(8,128)(2,1)S(1)} %get-tuple-element.11), channel_id=1, source_target_pairs={{16,0},{20,1},{24,2},{28,3},{17,4},{21,5},{25,6},{29,7},{18,8},{22... | collective-permute-start | bytes 196616 | tf_op jit(solution)/shard_map/ppermute | solution.py:411
  35.7 52.7 %collective-permute-start.5 = (bf16[128,256]{1,0:T(8,128)(2,1)S(1)}, bf16[128,256]{1,0:T(8,128)(2,1)S(1)}, u32[]{:S(2)}, u32[]{:S(2)}) collective-permute-start(bf16[128,256]{1,0:T(8,128)(2,1)S(1)} %get-tuple-element.11), channel_id=1, source_target_pairs={{0,0},{4,1},{8,2},{12,3},{1,4},{5,5},{9,6},{13,7},{2,8},{6,9},{10,... | collective-permute-start | bytes 196616 | tf_op jit(solution)/shard_map/ppermute | solution.py:411
  37.6 50.8 %collective-permute-start.4 = (bf16[8,80,256]{2,1,0:T(8,128)(2,1)}, bf16[8,80,256]{2,1,0:T(8,128)(2,1)S(1)}, u32[]{:S(2)}, u32[]{:S(2)}) collective-permute-start(bf16[8,80,256]{2,1,0:T(8,128)(2,1)} %all_to_all.5.recv_ref.refs_0_), channel_id=1, source_target_pairs={{0,3},{1,0},{2,1},{3,2},{4,7},{5,4},{6,5},{7,6},{8,11},{9,8},{10,9... | collective-permute-start | bytes 983048 | tf_op jit(solution)/shard_map/ppermute | solution.py:386
  39.9 48.5 %collective-permute-start.3 = (bf16[8,80,256]{2,1,0:T(8,128)(2,1)}, bf16[8,80,256]{2,1,0:T(8,128)(2,1)S(1)}, u32[]{:S(2)}, u32[]{:S(2)}) collective-permute-start(bf16[8,80,256]{2,1,0:T(8,128)(2,1)} %all_to_all.5.recv_ref.refs_0_), channel_id=1, source_target_pairs={{0,2},{1,3},{2,0},{3,1},{4,6},{5,7},{6,4},{7,5},{8,10},{9,11},{10,... | collective-permute-start | bytes 983048 | tf_op jit(solution)/shard_map/ppermute | solution.py:386
  39.9 48.5 %collective-permute-start.2 = (bf16[8,80,256]{2,1,0:T(8,128)(2,1)}, bf16[8,80,256]{2,1,0:T(8,128)(2,1)S(1)}, u32[]{:S(2)}, u32[]{:S(2)}) collective-permute-start(bf16[8,80,256]{2,1,0:T(8,128)(2,1)} %all_to_all.5.recv_ref.refs_0_), channel_id=1, source_target_pairs={{0,1},{1,2},{2,3},{3,0},{4,5},{5,6},{6,7},{7,4},{8,9},{9,10},{10,1... | collective-permute-start | bytes 983048 | tf_op jit(solution)/shard_map/ppermute | solution.py:386
  55.4 33.0 %copy-start = (bf16[8,80,256]{2,1,0:T(8,128)(2,1)S(1)}, bf16[8,80,256]{2,1,0:T(8,128)(2,1)}, u32[]{:S(2)}) copy-start(bf16[8,80,256]{2,1,0:T(8,128)(2,1)} %all_to_all.5.recv_ref.refs_0_) | copy-start | bytes 983044

commit v5 on v4

--- a/solution.py
+++ b/solution.py
@@ -166,21 +166,25 @@
 
 
 def diag_inverse(block):
-    size, width, ahead = block.shape[0], 8, 2
+    size, width, ahead = block.shape[0], 8, 3
     count = size // width
     shape = (width, size)
     sub, lane = iota(shape, 0), iota(shape, 1)
     spread = lambda x: jnp.broadcast_to(x, shape)
-    left = [block[q * width : (q + 1) * width, :] for q in range(count)]
-    right = [jnp.where(lane == sub + q * width, 1.0, 0.0).astype(F32) for q in range(count)]
+    work = [block[q * width : (q + 1) * width, :] for q in range(count)]
     columns = {}
     out = []
     for g in range(count):
-        rows = range(g, min(g + ahead + 1, count))
+        base, first = g * width, g + ahead + 1
+        rows = range(g, min(first, count))
         for q in rows:
-            for h in range(g, min(q, g + ahead - 1) + 1):
+            for h in range(g, min(q, g + 1) + 1):
                 if (q, h) not in columns:
-                    columns[q, h] = [spread(left[q][:, h * width + k : h * width + k + 1]) for k in range(width)]
+                    columns[q, h] = [spread(work[q][:, h * width + k : h * width + k + 1]) for k in range(width)]
+        pivot_lane = (lane >= base) & (lane < base + width)
+        for q in rows:
+            start = jnp.where(lane - base == sub, 1.0, 0.0) if q == g else 0.0
+            work[q] = jnp.where(pivot_lane, start, work[q])
         diag = jnp.ones(shape, F32)
         for i in range(width):
             own = spread(columns[g, g][i][i : i + 1, :])
@@ -189,31 +193,26 @@
             source = {q: columns[q, g][i] for q in rows}
             factor = {q: source[q] * inv for q in rows}
             factor[g] = jnp.where(sub > i, factor[g], 0.0)
-            for h in range(g, min(g + ahead, count)):
+            for h in range(g, min(g + 2, count)):
                 for k in range(i + 1 if h == g else 0, width):
                     value = spread(source[h][k : k + 1, :])
                     for q in rows:
                         if q >= h:
                             columns[q, h][k] = columns[q, h][k] - factor[q] * value
-            pivot_l, pivot_r = spread(left[g][i : i + 1, :]), spread(right[g][i : i + 1, :])
+            pivot = spread(work[g][i : i + 1, :])
             for q in rows:
-                left[q] = left[q] - factor[q] * pivot_l
-                right[q] = right[q] - factor[q] * pivot_r
-        scale = lax.rsqrt(diag)
-        pivot_l, pivot_r = left[g] * scale, right[g] * scale
-        out.append(pivot_r)
-        first = g + ahead + 1
+                work[q] = work[q] - factor[q] * pivot
+        scaled = work[g] * lax.rsqrt(diag)
+        out.append(jnp.where(lane < base + width, scaled, 0.0))
         if first < count:
-            high = [x.astype(BF16).astype(F32) for x in (pivot_l, pivot_r)]
-            low = [x - h for x, h in zip((pivot_l, pivot_r), high)]
-            zero = jnp.zeros_like(pivot_l)
-            lhs = jnp.concatenate([high[0], high[0], low[0], zero], axis=0).astype(BF16)
-            high, low = jnp.concatenate(high, axis=1), jnp.concatenate(low, axis=1)
-            rhs = jnp.concatenate([high, low, high, jnp.zeros_like(high)], axis=0).astype(BF16)
+            high = scaled.astype(BF16).astype(F32)
+            low = scaled - high
+            zero = jnp.zeros_like(high)
+            lhs = jnp.concatenate([high, high, low, zero], axis=0).astype(BF16)
+            rhs = jnp.concatenate([high, low, high, zero], axis=0).astype(BF16)
             gone = dot(lhs, rhs, TN)
             for q in range(first, count):
-                left[q] = left[q] - gone[q * width : (q + 1) * width, :size]
-                right[q] = right[q] - gone[q * width : (q + 1) * width, size:]
+                work[q] = jnp.where(pivot_lane, 0.0, work[q]) - gone[q * width : (q + 1) * width, :]
     return jnp.concatenate(out, axis=0)
 
 
@@ -222,11 +221,14 @@
     feats = cols_ref[...]
     half = half_norms(feats)
     half_row = as_row(half)
-    eye = iota((TILE, PANEL), 0) - iota((TILE, PANEL), 1)
-    for k in range(blocks):
-        rows = slice(k * TILE, (k + 1) * TILE)
-        block = rbf(feats[rows], half[rows], feats, half_row)
-        work_ref[rows, :] = block + jnp.where(eye == -k * TILE, noise_var, 0.0)
+    chunk = 2 * TILE
+    for top in range(0, PANEL, chunk):
+        rows, cols = slice(top, top + chunk), slice(top, PANEL)
+        block = rbf(feats[rows], half[rows], feats[cols], half_row[:, cols])
+        eye = iota(block.shape, 0) == iota(block.shape, 1)
+        work_ref[rows, cols] = block + jnp.where(eye, noise_var, 0.0)
+        if top:
+            work_ref[rows, :top] = jnp.zeros((chunk, top), F32)
     lane = iota((TILE, PANEL), 1)
 
     def step(k, carry):
@@ -238,8 +240,12 @@
         row = dot_split(split(inverse), split(work_ref[pl.ds(base, TILE), :]))
         out_ref[pl.ds(base, TILE), :] = jnp.where(lane < base + TILE, row, 0.0)
         high, low = split(row)
-        high_ref[...] = high
-        low_ref[...] = low
+        high_ref[:TILE, :] = high
+        high_ref[TILE : 2 * TILE, :] = low
+        high_ref[2 * TILE :, :] = high
+        low_ref[:TILE, :] = high
+        low_ref[TILE : 2 * TILE, :] = high
+        low_ref[2 * TILE :, :] = low
 
         for done in range(1, blocks):
 
@@ -247,8 +253,11 @@
             def _():
                 rest = slice(done * TILE, PANEL)
                 work_ref[rest, (done - 1) * TILE : done * TILE] = jnp.zeros((PANEL - done * TILE, TILE), F32)
-                lower = (high_ref[:, rest], low_ref[:, rest])
-                work_ref[rest, :] -= dot_split(lower, (high_ref[...], low_ref[...]), TN)
+                for top in range(done * TILE, PANEL, 2 * TILE):
+                    part = slice(top, min(top + 2 * TILE, PANEL))
+                    near, far = slice(0, done * TILE), slice(top, PANEL)
+                    work_ref[part, near] -= dot(low_ref[:, part], high_ref[:, near], TN)
+                    work_ref[part, far] -= dot(low_ref[:, part], high_ref[:, far], TN)
 
         return carry
 
@@ -261,8 +270,8 @@
         out_shape=jax.ShapeDtypeStruct((PANEL, PANEL), F32),
         scratch_shapes=[
             pltpu.VMEM((PANEL, PANEL), F32),
-            pltpu.VMEM((TILE, PANEL), BF16),
-            pltpu.VMEM((TILE, PANEL), BF16),
+            pltpu.VMEM((3 * TILE, PANEL), BF16),
+            pltpu.VMEM((3 * TILE, PANEL), BF16),
         ],
         compiler_params=pltpu.CompilerParams(vmem_limit_bytes=24 << 20),
         cost_estimate=pl.CostEstimate(flops=40 * 10**9, transcendentals=1 << 20, bytes_accessed=5 << 20),
@@ -428,10 +437,11 @@
     lead = sum_over(lead, "col", col_count)
     lead, received = lax.optimization_barrier((lead, received))
     parts = [received] + [shift(received, "col", d, col_count) for d in range(1, col_count)]
+    columns = lax.all_gather(lead[:TILE], "row", axis=0, tiled=True)
     if lead_tiles > 1:
+        lead, columns = lax.optimization_barrier((lead, columns))
         pieces, piece_tiles = next_tiles(lead[TILE : 2 * TILE], row_count, col_count)
-    columns = lax.all_gather(lead[:TILE], "row", axis=0, tiled=True)
-    if lead_tiles == 1:
+    else:
         pieces = [columns[PANEL + t * TILE : PANEL + (t + 1) * TILE] for t in range(PANEL // TILE)]
         piece_tiles = [jnp.int32(t) for t in range(PANEL // TILE)]
     inverse = make_inverse(columns[:PANEL])

time: 110 us -> 104 us (0.945)
  Pallas kernels: 61 us -> 56.8 us
  blocking collectives: 24.7 us -> 21.5 us
  starting transfers between devices: 11.6 us -> 13.6 us
    pallas_call x1, Pallas kernels: 33 us -> 28.9 us  [make_inverse(): pl.pallas_call(chol_kernel, out_shape=jax.ShapeDtypeStruct((PANEL, PANEL)...]
    all_gather x1, blocking collectives: 14.2 us -> 11 us  [per_device(): columns = lax.all_gather(lead[:TILE], 'row', axis=0, tiled=True)]
    ppermute x3, starting transfers between devices: 3.53 us -> 5.52 us  [shift(): lax.ppermute(value, axis, [(i, (i + distance) % size) for i in range(size)])]
  transfers between devices with their start and end apart: 7 -> 7, of which waited for: 2 -> 2; matrix products, arithmetic and copies ran while one was open for 0% -> 0% of each run, Pallas kernels for 30% -> 28%
where the time goes in v5:
time: 104 us
  Pallas kernels  56.8 us (55%)
  blocking collectives  21.5 us (21%)
  starting transfers between devices  13.6 us (13%)
  waiting for transfers between devices  9.94 us (10%)
  other arithmetic  1.05 us (1%)
    pallas_call x1, Pallas kernels, make_inverse(): pl.pallas_call(chol_kernel, out_shape=jax.ShapeDtypeStruct((PANEL, PANEL)...  28.9 us
    pallas_call x1, Pallas kernels, make_outputs(): pl.pallas_call(functools.partial(panel_kernel, share, row_count, col_coun...  20.5 us
    all_gather x1, blocking collectives, per_device(): columns = lax.all_gather(lead[:TILE], 'row', axis=0, tiled=True)  11 us
    all_to_all x1, blocking collectives, per_device(): lax.all_to_all(bucket, 'row', split_axis=0, concat_axis=0, tiled=True)  10.5 us
    ppermute x2, waiting for transfers between devices, exchange(): return lax.ppermute(value, axis, [(i, i ^ step) for i in range(size)])  9.93 us
    ppermute x2, starting transfers between devices, next_tiles(): pieces.append(lax.ppermute(tile, ('row', 'col'), pairs))  5.6 us
    pallas_call x1, Pallas kernels, make_features(): pl.pallas_call(functools.partial(feature_kernel, share, row_count), out_s...  5.55 us
    ppermute x3, starting transfers between devices, shift(): lax.ppermute(value, axis, [(i, (i + distance) % size) for i in range(size)])  5.52 us
  transfers between devices with their start and end apart: 7, of which 2 were waited for; matrix products, arithmetic and copies ran while one was open for 0% of the time, Pallas kernels for 28%

profile of v5, /device:TPU:11, one launch (start us, length us, event | category | flops | bytes accessed | tf_op | source)
XLA Modules:
  0.0 103.7 jit_solution(4879133173601488088)
XLA Ops:
  0.6 5.6 %features.1 = bf16[8,80,256]{2,1,0:T(8,128)(2,1)S(1)} custom-call(s32[1,512]{1,0:T(1,128)} %bitcast.10, bf16[512,768]{1,0:T(8,128)(2,1)} %img_ref.1, bf16[768,2048]{1,0:T(8,128)(2,1)} %win_ref.1, f32[1,2048]{1,0:T(1,128)} %bitcast.9, bf16[2048,256]{1,0:T(8,128)(2,1)} %wout_ref.1, f32[1,256]{1,0:T(1,128)} %bitcast.11), custom_call_target="tpu_custom_call" | custom-call | tf_op jit(solution)/shard_map/features/pallas_call | solution.py:115
  6.2 10.5 %all_to_all.5.recv_ref.refs_0_ = bf16[8,80,256]{2,1,0:T(8,128)(2,1)} all-to-all(bf16[8,80,256]{2,1,0:T(8,128)(2,1)S(1)} %features.1), channel_id=1, replica_groups=mesh['row'=8,'col'=4] {'row'}, dimensions={0} | all-to-all | bytes 655360 | tf_op jit(solution)/shard_map/all_to_all | solution.py:435
  16.6 1.9 %lead.1 = bf16[256,256]{1,0:T(8,128)(2,1)} custom-call(bf16[8,80,256]{2,1,0:T(8,128)(2,1)} %all_to_all.5.recv_ref.refs_0_), custom_call_target="tpu_custom_call" | custom-call | tf_op jit(solution)/shard_map/lead/pallas_call | solution.py:161
  18.5 0.2 collective-permute-start
  18.7 4.5 %collective-permute-done = bf16[256,256]{1,0:T(8,128)(2,1)S(1)} collective-permute-done((bf16[256,256]{1,0:T(8,128)(2,1)}, bf16[256,256]{1,0:T(8,128)(2,1)S(1)}, u32[]{:S(2)}, u32[]{:S(2)}) %collective-permute-start) | collective-permute-done | bytes 131104 | tf_op jit(solution)/shard_map/ppermute | solution.py:399
  23.2 0.9 add.28
  24.2 2.4 %collective-permute-start.1 = (bf16[256,256]{1,0:T(8,128)(2,1)S(1)}, bf16[256,256]{1,0:T(8,128)(2,1)S(1)}, u32[]{:S(2)}, u32[]{:S(2)}) collective-permute-start(bf16[256,256]{1,0:T(8,128)(2,1)S(1)} %add.28), channel_id=1, source_target_pairs={{0,2},{1,3},{2,0},{3,1},{4,6},{5,7},{6,4},{7,5},{8,10},{9,11},{10,... | collective-permute-start | bytes 393224 | tf_op jit(solution)/shard_map/ppermute | solution.py:399
  26.5 0.1 pad_add_fusion.place_ref
  26.6 5.4 %collective-permute-done.1 = bf16[256,256]{1,0:T(8,128)(2,1)S(1)} collective-permute-done((bf16[256,256]{1,0:T(8,128)(2,1)S(1)}, bf16[256,256]{1,0:T(8,128)(2,1)S(1)}, u32[]{:S(2)}, u32[]{:S(2)}) %collective-permute-start.1) | collective-permute-done | bytes 131104 | tf_op jit(solution)/shard_map/ppermute | solution.py:399
  32.0 0.5 collective-permute-start.4
  32.5 2.7 %collective-permute-start.3 = (bf16[8,80,256]{2,1,0:T(8,128)(2,1)}, bf16[8,80,256]{2,1,0:T(8,128)(2,1)S(1)}, u32[]{:S(2)}, u32[]{:S(2)}) collective-permute-start(bf16[8,80,256]{2,1,0:T(8,128)(2,1)} %all_to_all.5.recv_ref.refs_0_), channel_id=1, source_target_pairs={{0,2},{1,3},{2,0},{3,1},{4,6},{5,7},{6,4},{7,5},{8,10},{9,11},{10,... | collective-permute-start | bytes 983048 | tf_op jit(solution)/shard_map/ppermute | solution.py:395
  35.3 2.3 %collective-permute-start.2 = (bf16[8,80,256]{2,1,0:T(8,128)(2,1)}, bf16[8,80,256]{2,1,0:T(8,128)(2,1)S(1)}, u32[]{:S(2)}, u32[]{:S(2)}) collective-permute-start(bf16[8,80,256]{2,1,0:T(8,128)(2,1)} %all_to_all.5.recv_ref.refs_0_), channel_id=1, source_target_pairs={{0,1},{1,2},{2,3},{3,0},{4,5},{5,6},{6,7},{7,4},{8,9},{9,10},{10,1... | collective-permute-start | bytes 983048 | tf_op jit(solution)/shard_map/ppermute | solution.py:395
  37.6 11.0 %all_gather.3.cols_ref.refs_6_ = bf16[1024,256]{1,0:T(8,128)(2,1)S(1)} all-gather(bf16[128,256]{1,0:T(8,128)(2,1)S(1)} %slice.6), channel_id=1, replica_groups=mesh['row'=8,'col'=4] {'row'}, dimensions={0}, use_global_device_ids=true | all-gather | bytes 589824 | tf_op jit(solution)/shard_map/all_gather | solution.py:440
  48.6 0.0 copy-start
  48.6 1.6 %collective-permute-start.6 = (bf16[128,256]{1,0:T(8,128)(2,1)S(1)}, bf16[128,256]{1,0:T(8,128)(2,1)S(1)}, u32[]{:S(2)}, u32[]{:S(2)}) collective-permute-start(bf16[128,256]{1,0:T(8,128)(2,1)S(1)} %slice.7), channel_id=1, source_target_pairs={{16,0},{20,1},{24,2},{28,3},{17,4},{21,5},{25,6},{29,7},{18,8},{22... | collective-permute-start | bytes 196616 | tf_op jit(solution)/shard_map/ppermute | solution.py:420
  50.2 4.0 %collective-permute-start.5 = (bf16[128,256]{1,0:T(8,128)(2,1)S(1)}, bf16[128,256]{1,0:T(8,128)(2,1)S(1)}, u32[]{:S(2)}, u32[]{:S(2)}) collective-permute-start(bf16[128,256]{1,0:T(8,128)(2,1)S(1)} %slice.7), channel_id=1, source_target_pairs={{0,0},{4,1},{8,2},{12,3},{1,4},{5,5},{9,6},{13,7},{2,8},{6,9},{10,... | collective-permute-start | bytes 196616 | tf_op jit(solution)/shard_map/ppermute | solution.py:420
  54.2 28.9 %cholesky.1.refs_7_ = f32[1024,1024]{1,0:T(8,128)S(1)} custom-call(bf16[1024,256]{1,0:T(8,128)(2,1)S(1)} %all_gather.3.cols_ref.refs_6_), custom_call_target="tpu_custom_call" | custom-call | flops 40000000000 | bytes 5242880 | tf_op jit(solution)/shard_map/cholesky/pallas_call | solution.py:268
  83.1 0.0 collective-permute-done.6.refs_5_
  83.1 0.0 collective-permute-done.5.refs_4_
  83.1 0.0 collective-permute-done.4.refs_3_
  83.1 0.0 collective-permute-done.3.refs_2_
  83.1 0.0 collective-permute-done.2.refs_1_
  83.2 0.0 copy-done
  83.2 20.5 %panels.1 = (f32[4096,128]{1,0:T(8,128)}, f32[4096,128]{1,0:T(8,128)}) custom-call(s32[4]{0:T(128)S(1)} %pad_add_fusion.place_ref, bf16[8,80,256]{2,1,0:T(8,128)(2,1)S(1)} %copy-done, bf16[8,80,256]{2,1,0:T(8,128)(2,1)S(1)} %collective-permute-done.2.refs_1_, bf16[8,80,256]{2,1,0:T(8,128)(2,1)S(1)} %collective-permute-done.3.refs_2_, ...), custom_call_target="tpu_custom_call" | custom-call | tf_op jit(solution)/shard_map/panels/pallas_call | solution.py:372
  (3 shorter events, 0.0 us)
Async XLA Ops:
  18.5 4.7 %collective-permute-start = (bf16[256,256]{1,0:T(8,128)(2,1)}, bf16[256,256]{1,0:T(8,128)(2,1)S(1)}, u32[]{:S(2)}, u32[]{:S(2)}) collective-permute-start(bf16[256,256]{1,0:T(8,128)(2,1)} %lead.1), channel_id=1, source_target_pairs={{0,1},{1,0},{2,3},{3,2},{4,5},{5,4},{6,7},{7,6},{8,9},{9,8},{10,11... | collective-permute-start | bytes 393224 | tf_op jit(solution)/shard_map/ppermute | solution.py:399
  24.2 7.8 %collective-permute-start.1 = (bf16[256,256]{1,0:T(8,128)(2,1)S(1)}, bf16[256,256]{1,0:T(8,128)(2,1)S(1)}, u32[]{:S(2)}, u32[]{:S(2)}) collective-permute-start(bf16[256,256]{1,0:T(8,128)(2,1)S(1)} %add.28), channel_id=1, source_target_pairs={{0,2},{1,3},{2,0},{3,1},{4,6},{5,7},{6,4},{7,5},{8,10},{9,11},{10,... | collective-permute-start | bytes 393224 | tf_op jit(solution)/shard_map/ppermute | solution.py:399
  32.0 51.1 %collective-permute-start.4 = (bf16[8,80,256]{2,1,0:T(8,128)(2,1)}, bf16[8,80,256]{2,1,0:T(8,128)(2,1)S(1)}, u32[]{:S(2)}, u32[]{:S(2)}) collective-permute-start(bf16[8,80,256]{2,1,0:T(8,128)(2,1)} %all_to_all.5.recv_ref.refs_0_), channel_id=1, source_target_pairs={{0,3},{1,0},{2,1},{3,2},{4,7},{5,4},{6,5},{7,6},{8,11},{9,8},{10,9... | collective-permute-start | bytes 983048 | tf_op jit(solution)/shard_map/ppermute | solution.py:395
  32.5 50.6 %collective-permute-start.3 = (bf16[8,80,256]{2,1,0:T(8,128)(2,1)}, bf16[8,80,256]{2,1,0:T(8,128)(2,1)S(1)}, u32[]{:S(2)}, u32[]{:S(2)}) collective-permute-start(bf16[8,80,256]{2,1,0:T(8,128)(2,1)} %all_to_all.5.recv_ref.refs_0_), channel_id=1, source_target_pairs={{0,2},{1,3},{2,0},{3,1},{4,6},{5,7},{6,4},{7,5},{8,10},{9,11},{10,... | collective-permute-start | bytes 983048 | tf_op jit(solution)/shard_map/ppermute | solution.py:395
  35.3 47.9 %collective-permute-start.2 = (bf16[8,80,256]{2,1,0:T(8,128)(2,1)}, bf16[8,80,256]{2,1,0:T(8,128)(2,1)S(1)}, u32[]{:S(2)}, u32[]{:S(2)}) collective-permute-start(bf16[8,80,256]{2,1,0:T(8,128)(2,1)} %all_to_all.5.recv_ref.refs_0_), channel_id=1, source_target_pairs={{0,1},{1,2},{2,3},{3,0},{4,5},{5,6},{6,7},{7,4},{8,9},{9,10},{10,1... | collective-permute-start | bytes 983048 | tf_op jit(solution)/shard_map/ppermute | solution.py:395
  48.6 34.6 %copy-start = (bf16[8,80,256]{2,1,0:T(8,128)(2,1)S(1)}, bf16[8,80,256]{2,1,0:T(8,128)(2,1)}, u32[]{:S(2)}) copy-start(bf16[8,80,256]{2,1,0:T(8,128)(2,1)} %all_to_all.5.recv_ref.refs_0_) | copy-start | bytes 983044
  48.6 34.5 %collective-permute-start.6 = (bf16[128,256]{1,0:T(8,128)(2,1)S(1)}, bf16[128,256]{1,0:T(8,128)(2,1)S(1)}, u32[]{:S(2)}, u32[]{:S(2)}) collective-permute-start(bf16[128,256]{1,0:T(8,128)(2,1)S(1)} %slice.7), channel_id=1, source_target_pairs={{16,0},{20,1},{24,2},{28,3},{17,4},{21,5},{25,6},{29,7},{18,8},{22... | collective-permute-start | bytes 196616 | tf_op jit(solution)/shard_map/ppermute | solution.py:420
  50.2 32.9 %collective-permute-start.5 = (bf16[128,256]{1,0:T(8,128)(2,1)S(1)}, bf16[128,256]{1,0:T(8,128)(2,1)S(1)}, u32[]{:S(2)}, u32[]{:S(2)}) collective-permute-start(bf16[128,256]{1,0:T(8,128)(2,1)S(1)} %slice.7), channel_id=1, source_target_pairs={{0,0},{4,1},{8,2},{12,3},{1,4},{5,5},{9,6},{13,7},{2,8},{6,9},{10,... | collective-permute-start | bytes 196616 | tf_op jit(solution)/shard_map/ppermute | solution.py:420

commit v6 on v5

--- a/solution.py
+++ b/solution.py
@@ -9,7 +9,7 @@
 
 TILE = 128
 PANEL = 1024
-META = 16
+META = 8
 F32 = jnp.float32
 BF16 = jnp.bfloat16
 NN = (((1,), (0,)), ((), ()))
@@ -62,7 +62,9 @@
 ):
     step = pl.program_id(0)
     preact = dot(img_ref[...], win_ref[...]) + bias_ref[...]
-    hidden = 0.5 * preact * (1.0 + jnp.tanh(0.7978845608 * (preact + 0.044715 * preact * preact * preact)))
+    inner = preact * (0.7978845608 + 0.7978845608 * 0.044715 * preact * preact)
+    half = 0.5 * preact
+    hidden = half + half * jnp.tanh(inner)
     part = dot(hidden.astype(BF16), wout_ref[...])
 
     @pl.when(step == 0)
@@ -316,7 +318,19 @@
         own_half = half_norms(own_feats)
         own_half_ref[...] = jnp.broadcast_to(as_row(own_half), (8, width))
         cross = rbf(own_feats, own_half, cols_ref[...], half_row)
-        solved = dot_split(split(dot_split(split(cross), inverse, NT)), inverse)
+        block = 2 * TILE
+        cut = lambda pair, rows, cols: (pair[0][rows, cols], pair[1][rows, cols])
+        cross = split(cross)
+        halfway = []
+        for n in range(0, PANEL, block):
+            here, upto = slice(n, n + block), slice(0, n + block)
+            halfway.append(dot_split(cut(cross, slice(None), upto), cut(inverse, here, upto), NT))
+        halfway = split(jnp.concatenate(halfway, axis=1))
+        solved = []
+        for n in range(0, PANEL, block):
+            here, below = slice(n, n + block), slice(n, PANEL)
+            solved.append(dot_split(cut(halfway, slice(None), below), cut(inverse, below, here)))
+        solved = jnp.concatenate(solved, axis=1)
         right = jnp.concatenate(own + [solved], axis=0)
         high, low = split(right.T)
         high_ref[0:PANEL, :] = high

time: 104 us -> 102 us (0.981)
  Pallas kernels: 56.8 us -> 55.5 us
    pallas_call x1, Pallas kernels: 20.5 us -> 19.2 us  [make_outputs(): pl.pallas_call(functools.partial(panel_kernel, share, row_count, col_coun...]
where the time goes in v6:
time: 102 us
  Pallas kernels  55.5 us (54%)
  blocking collectives  21.3 us (21%)
  starting transfers between devices  13.5 us (13%)
  waiting for transfers between devices  10.1 us (10%)
  other arithmetic  1.05 us (1%)
    pallas_call x1, Pallas kernels, make_inverse(): pl.pallas_call(chol_kernel, out_shape=jax.ShapeDtypeStruct((PANEL, PANEL)...  28.9 us
    pallas_call x1, Pallas kernels, make_outputs(): pl.pallas_call(functools.partial(panel_kernel, share, row_count, col_coun...  19.2 us
    all_gather x1, blocking collectives, per_device(): columns = lax.all_gather(lead[:TILE], 'row', axis=0, tiled=True)  11.1 us
    all_to_all x1, blocking collectives, per_device(): lax.all_to_all(bucket, 'row', split_axis=0, concat_axis=0, tiled=True)  10.2 us
    ppermute x2, waiting for transfers between devices, exchange(): return lax.ppermute(value, axis, [(i, i ^ step) for i in range(size)])  10.1 us
    pallas_call x1, Pallas kernels, make_features(): pl.pallas_call(functools.partial(feature_kernel, share, row_count), out_s...  5.53 us
    ppermute x3, starting transfers between devices, shift(): lax.ppermute(value, axis, [(i, (i + distance) % size) for i in range(size)])  5.52 us
    ppermute x2, starting transfers between devices, next_tiles(): pieces.append(lax.ppermute(tile, ('row', 'col'), pairs))  5.42 us
  transfers between devices with their start and end apart: 7, of which 2 were waited for; matrix products, arithmetic and copies ran while one was open for 0% of the time, Pallas kernels for 28%

profile of v6, /device:TPU:11, one launch (start us, length us, event | category | flops | bytes accessed | tf_op | source)
XLA Modules:
  0.0 102.2 jit_solution(4987868763197573283)
XLA Ops:
  0.6 5.5 %features.1 = bf16[8,72,256]{2,1,0:T(8,128)(2,1)S(1)} custom-call(s32[1,512]{1,0:T(1,128)} %bitcast.10, bf16[512,768]{1,0:T(8,128)(2,1)} %img_ref.1, bf16[768,2048]{1,0:T(8,128)(2,1)} %win_ref.1, f32[1,2048]{1,0:T(1,128)} %bitcast.9, bf16[2048,256]{1,0:T(8,128)(2,1)} %wout_ref.1, f32[1,256]{1,0:T(1,128)} %bitcast.11), custom_call_target="tpu_custom_call" | custom-call | tf_op jit(solution)/shard_map/features/pallas_call | solution.py:117
  6.2 10.2 %all_to_all.5.recv_ref.refs_0_ = bf16[8,72,256]{2,1,0:T(8,128)(2,1)} all-to-all(bf16[8,72,256]{2,1,0:T(8,128)(2,1)S(1)} %features.1), channel_id=1, replica_groups=mesh['row'=8,'col'=4] {'row'}, dimensions={0} | all-to-all | bytes 589824 | tf_op jit(solution)/shard_map/all_to_all | solution.py:449
  16.4 1.9 %lead.1 = bf16[256,256]{1,0:T(8,128)(2,1)} custom-call(bf16[8,72,256]{2,1,0:T(8,128)(2,1)} %all_to_all.5.recv_ref.refs_0_), custom_call_target="tpu_custom_call" | custom-call | tf_op jit(solution)/shard_map/lead/pallas_call | solution.py:163
  18.2 0.2 collective-permute-start
  18.4 4.6 %collective-permute-done = bf16[256,256]{1,0:T(8,128)(2,1)S(1)} collective-permute-done((bf16[256,256]{1,0:T(8,128)(2,1)}, bf16[256,256]{1,0:T(8,128)(2,1)S(1)}, u32[]{:S(2)}, u32[]{:S(2)}) %collective-permute-start) | collective-permute-done | bytes 131104 | tf_op jit(solution)/shard_map/ppermute | solution.py:413
  23.0 0.9 add.28
  24.0 2.4 %collective-permute-start.1 = (bf16[256,256]{1,0:T(8,128)(2,1)S(1)}, bf16[256,256]{1,0:T(8,128)(2,1)S(1)}, u32[]{:S(2)}, u32[]{:S(2)}) collective-permute-start(bf16[256,256]{1,0:T(8,128)(2,1)S(1)} %add.28), channel_id=1, source_target_pairs={{0,2},{1,3},{2,0},{3,1},{4,6},{5,7},{6,4},{7,5},{8,10},{9,11},{10,... | collective-permute-start | bytes 393224 | tf_op jit(solution)/shard_map/ppermute | solution.py:413
  26.3 0.1 pad_add_fusion.place_ref
  26.4 5.5 %collective-permute-done.1 = bf16[256,256]{1,0:T(8,128)(2,1)S(1)} collective-permute-done((bf16[256,256]{1,0:T(8,128)(2,1)S(1)}, bf16[256,256]{1,0:T(8,128)(2,1)S(1)}, u32[]{:S(2)}, u32[]{:S(2)}) %collective-permute-start.1) | collective-permute-done | bytes 131104 | tf_op jit(solution)/shard_map/ppermute | solution.py:413
  31.9 0.4 collective-permute-start.4
  32.3 2.8 %collective-permute-start.3 = (bf16[8,72,256]{2,1,0:T(8,128)(2,1)}, bf16[8,72,256]{2,1,0:T(8,128)(2,1)S(1)}, u32[]{:S(2)}, u32[]{:S(2)}) collective-permute-start(bf16[8,72,256]{2,1,0:T(8,128)(2,1)} %all_to_all.5.recv_ref.refs_0_), channel_id=1, source_target_pairs={{0,2},{1,3},{2,0},{3,1},{4,6},{5,7},{6,4},{7,5},{8,10},{9,11},{10,... | collective-permute-start | bytes 884744 | tf_op jit(solution)/shard_map/ppermute | solution.py:409
  35.2 2.3 %collective-permute-start.2 = (bf16[8,72,256]{2,1,0:T(8,128)(2,1)}, bf16[8,72,256]{2,1,0:T(8,128)(2,1)S(1)}, u32[]{:S(2)}, u32[]{:S(2)}) collective-permute-start(bf16[8,72,256]{2,1,0:T(8,128)(2,1)} %all_to_all.5.recv_ref.refs_0_), channel_id=1, source_target_pairs={{0,1},{1,2},{2,3},{3,0},{4,5},{5,6},{6,7},{7,4},{8,9},{9,10},{10,1... | collective-permute-start | bytes 884744 | tf_op jit(solution)/shard_map/ppermute | solution.py:409
  37.5 11.1 %all_gather.3.cols_ref.refs_6_ = bf16[1024,256]{1,0:T(8,128)(2,1)S(1)} all-gather(bf16[128,256]{1,0:T(8,128)(2,1)S(1)} %slice.6), channel_id=1, replica_groups=mesh['row'=8,'col'=4] {'row'}, dimensions={0}, use_global_device_ids=true | all-gather | bytes 589824 | tf_op jit(solution)/shard_map/all_gather | solution.py:454
  48.6 0.0 copy-start
  48.6 1.6 %collective-permute-start.6 = (bf16[128,256]{1,0:T(8,128)(2,1)S(1)}, bf16[128,256]{1,0:T(8,128)(2,1)S(1)}, u32[]{:S(2)}, u32[]{:S(2)}) collective-permute-start(bf16[128,256]{1,0:T(8,128)(2,1)S(1)} %slice.7), channel_id=1, source_target_pairs={{16,0},{20,1},{24,2},{28,3},{17,4},{21,5},{25,6},{29,7},{18,8},{22... | collective-permute-start | bytes 196616 | tf_op jit(solution)/shard_map/ppermute | solution.py:434
  50.2 3.8 %collective-permute-start.5 = (bf16[128,256]{1,0:T(8,128)(2,1)S(1)}, bf16[128,256]{1,0:T(8,128)(2,1)S(1)}, u32[]{:S(2)}, u32[]{:S(2)}) collective-permute-start(bf16[128,256]{1,0:T(8,128)(2,1)S(1)} %slice.7), channel_id=1, source_target_pairs={{0,0},{4,1},{8,2},{12,3},{1,4},{5,5},{9,6},{13,7},{2,8},{6,9},{10,... | collective-permute-start | bytes 196616 | tf_op jit(solution)/shard_map/ppermute | solution.py:434
  54.0 28.9 %cholesky.1.refs_7_ = f32[1024,1024]{1,0:T(8,128)S(1)} custom-call(bf16[1024,256]{1,0:T(8,128)(2,1)S(1)} %all_gather.3.cols_ref.refs_6_), custom_call_target="tpu_custom_call" | custom-call | flops 40000000000 | bytes 5242880 | tf_op jit(solution)/shard_map/cholesky/pallas_call | solution.py:270
  82.9 0.0 collective-permute-done.6.refs_5_
  82.9 0.0 collective-permute-done.5.refs_4_
  82.9 0.0 collective-permute-done.4.refs_3_
  82.9 0.0 collective-permute-done.3.refs_2_
  83.0 0.0 collective-permute-done.2.refs_1_
  83.0 0.0 copy-done
  83.0 19.2 %panels.1 = (f32[4096,128]{1,0:T(8,128)}, f32[4096,128]{1,0:T(8,128)}) custom-call(s32[4]{0:T(128)S(1)} %pad_add_fusion.place_ref, bf16[8,72,256]{2,1,0:T(8,128)(2,1)S(1)} %copy-done, bf16[8,72,256]{2,1,0:T(8,128)(2,1)S(1)} %collective-permute-done.2.refs_1_, bf16[8,72,256]{2,1,0:T(8,128)(2,1)S(1)} %collective-permute-done.3.refs_2_, ...), custom_call_target="tpu_custom_call" | custom-call | tf_op jit(solution)/shard_map/panels/pallas_call | solution.py:386
  (3 shorter events, 0.0 us)
Async XLA Ops:
  18.2 4.8 %collective-permute-start = (bf16[256,256]{1,0:T(8,128)(2,1)}, bf16[256,256]{1,0:T(8,128)(2,1)S(1)}, u32[]{:S(2)}, u32[]{:S(2)}) collective-permute-start(bf16[256,256]{1,0:T(8,128)(2,1)} %lead.1), channel_id=1, source_target_pairs={{0,1},{1,0},{2,3},{3,2},{4,5},{5,4},{6,7},{7,6},{8,9},{9,8},{10,11... | collective-permute-start | bytes 393224 | tf_op jit(solution)/shard_map/ppermute | solution.py:413
  24.0 7.9 %collective-permute-start.1 = (bf16[256,256]{1,0:T(8,128)(2,1)S(1)}, bf16[256,256]{1,0:T(8,128)(2,1)S(1)}, u32[]{:S(2)}, u32[]{:S(2)}) collective-permute-start(bf16[256,256]{1,0:T(8,128)(2,1)S(1)} %add.28), channel_id=1, source_target_pairs={{0,2},{1,3},{2,0},{3,1},{4,6},{5,7},{6,4},{7,5},{8,10},{9,11},{10,... | collective-permute-start | bytes 393224 | tf_op jit(solution)/shard_map/ppermute | solution.py:413
  31.9 51.0 %collective-permute-start.4 = (bf16[8,72,256]{2,1,0:T(8,128)(2,1)}, bf16[8,72,256]{2,1,0:T(8,128)(2,1)S(1)}, u32[]{:S(2)}, u32[]{:S(2)}) collective-permute-start(bf16[8,72,256]{2,1,0:T(8,128)(2,1)} %all_to_all.5.recv_ref.refs_0_), channel_id=1, source_target_pairs={{0,3},{1,0},{2,1},{3,2},{4,7},{5,4},{6,5},{7,6},{8,11},{9,8},{10,9... | collective-permute-start | bytes 884744 | tf_op jit(solution)/shard_map/ppermute | solution.py:409
  32.3 50.6 %collective-permute-start.3 = (bf16[8,72,256]{2,1,0:T(8,128)(2,1)}, bf16[8,72,256]{2,1,0:T(8,128)(2,1)S(1)}, u32[]{:S(2)}, u32[]{:S(2)}) collective-permute-start(bf16[8,72,256]{2,1,0:T(8,128)(2,1)} %all_to_all.5.recv_ref.refs_0_), channel_id=1, source_target_pairs={{0,2},{1,3},{2,0},{3,1},{4,6},{5,7},{6,4},{7,5},{8,10},{9,11},{10,... | collective-permute-start | bytes 884744 | tf_op jit(solution)/shard_map/ppermute | solution.py:409
  35.2 47.8 %collective-permute-start.2 = (bf16[8,72,256]{2,1,0:T(8,128)(2,1)}, bf16[8,72,256]{2,1,0:T(8,128)(2,1)S(1)}, u32[]{:S(2)}, u32[]{:S(2)}) collective-permute-start(bf16[8,72,256]{2,1,0:T(8,128)(2,1)} %all_to_all.5.recv_ref.refs_0_), channel_id=1, source_target_pairs={{0,1},{1,2},{2,3},{3,0},{4,5},{5,6},{6,7},{7,4},{8,9},{9,10},{10,1... | collective-permute-start | bytes 884744 | tf_op jit(solution)/shard_map/ppermute | solution.py:409
  48.6 34.4 %copy-start = (bf16[8,72,256]{2,1,0:T(8,128)(2,1)S(1)}, bf16[8,72,256]{2,1,0:T(8,128)(2,1)}, u32[]{:S(2)}) copy-start(bf16[8,72,256]{2,1,0:T(8,128)(2,1)} %all_to_all.5.recv_ref.refs_0_) | copy-start | bytes 884740
  48.6 34.3 %collective-permute-start.6 = (bf16[128,256]{1,0:T(8,128)(2,1)S(1)}, bf16[128,256]{1,0:T(8,128)(2,1)S(1)}, u32[]{:S(2)}, u32[]{:S(2)}) collective-permute-start(bf16[128,256]{1,0:T(8,128)(2,1)S(1)} %slice.7), channel_id=1, source_target_pairs={{16,0},{20,1},{24,2},{28,3},{17,4},{21,5},{25,6},{29,7},{18,8},{22... | collective-permute-start | bytes 196616 | tf_op jit(solution)/shard_map/ppermute | solution.py:434
  50.2 32.7 %collective-permute-start.5 = (bf16[128,256]{1,0:T(8,128)(2,1)S(1)}, bf16[128,256]{1,0:T(8,128)(2,1)S(1)}, u32[]{:S(2)}, u32[]{:S(2)}) collective-permute-start(bf16[128,256]{1,0:T(8,128)(2,1)S(1)} %slice.7), channel_id=1, source_target_pairs={{0,0},{4,1},{8,2},{12,3},{1,4},{5,5},{9,6},{13,7},{2,8},{6,9},{10,... | collective-permute-start | bytes 196616 | tf_op jit(solution)/shard_map/ppermute | solution.py:434

commit v7 on v6

--- a/solution.py
+++ b/solution.py
@@ -39,6 +39,15 @@
 def dot_split(left, right, dims=NN):
     return dot(left[0], right[0], dims) + (
         dot(left[0], right[1], dims) + dot(left[1], right[0], dims)
+    )
+
+
+def dot_stacked(left, right, dims=NN):
+    side = dims[0][1][0]
+    return dot(
+        jnp.concatenate([left[0], left[0], left[1]], axis=1),
+        jnp.concatenate([right[0], right[1], right[0]], axis=side),
+        dims,
     )
 
 
@@ -218,7 +227,7 @@
     return jnp.concatenate(out, axis=0)
 
 
-def chol_kernel(cols_ref, out_ref, work_ref, high_ref, low_ref):
+def chol_kernel(cols_ref, out_ref, work_ref, stack_ref):
     blocks = PANEL // TILE
     feats = cols_ref[...]
     half = half_norms(feats)
@@ -239,15 +248,12 @@
         work_ref[pl.ds(base, TILE), pl.ds(base, TILE)] = jnp.where(
             iota((TILE, TILE), 0) == iota((TILE, TILE), 1), 1.0, 0.0
         )
-        row = dot_split(split(inverse), split(work_ref[pl.ds(base, TILE), :]))
+        row = dot_stacked(split(inverse), split(work_ref[pl.ds(base, TILE), :]))
         out_ref[pl.ds(base, TILE), :] = jnp.where(lane < base + TILE, row, 0.0)
         high, low = split(row)
-        high_ref[:TILE, :] = high
-        high_ref[TILE : 2 * TILE, :] = low
-        high_ref[2 * TILE :, :] = high
-        low_ref[:TILE, :] = high
-        low_ref[TILE : 2 * TILE, :] = high
-        low_ref[2 * TILE :, :] = low
+        stack_ref[:TILE, :] = high
+        stack_ref[TILE : 2 * TILE, :] = low
+        stack_ref[2 * TILE :, :] = high
 
         for done in range(1, blocks):
 
@@ -255,11 +261,13 @@
             def _():
                 rest = slice(done * TILE, PANEL)
                 work_ref[rest, (done - 1) * TILE : done * TILE] = jnp.zeros((PANEL - done * TILE, TILE), F32)
-                for top in range(done * TILE, PANEL, 2 * TILE):
-                    part = slice(top, min(top + 2 * TILE, PANEL))
-                    near, far = slice(0, done * TILE), slice(top, PANEL)
-                    work_ref[part, near] -= dot(low_ref[:, part], high_ref[:, near], TN)
-                    work_ref[part, far] -= dot(low_ref[:, part], high_ref[:, far], TN)
+                turned = [x[:, rest].T for x in (high, low)]
+                lower = jnp.concatenate([turned[0], turned[0], turned[1]], axis=1)
+                for n in range(0, PANEL, 2 * TILE):
+                    cols = slice(n, n + 2 * TILE)
+                    stop = PANEL if n < done * TILE else n + 2 * TILE
+                    mine = lower[: stop - done * TILE]
+                    work_ref[done * TILE : stop, cols] -= dot(mine, stack_ref[:, cols])
 
         return carry
 
@@ -272,7 +280,6 @@
         out_shape=jax.ShapeDtypeStruct((PANEL, PANEL), F32),
         scratch_shapes=[
             pltpu.VMEM((PANEL, PANEL), F32),
-            pltpu.VMEM((3 * TILE, PANEL), BF16),
             pltpu.VMEM((3 * TILE, PANEL), BF16),
         ],
         compiler_params=pltpu.CompilerParams(vmem_limit_bytes=24 << 20),
@@ -324,12 +331,12 @@
         halfway = []
         for n in range(0, PANEL, block):
             here, upto = slice(n, n + block), slice(0, n + block)
-            halfway.append(dot_split(cut(cross, slice(None), upto), cut(inverse, here, upto), NT))
+            halfway.append(dot_stacked(cut(cross, slice(None), upto), cut(inverse, here, upto), NT))
         halfway = split(jnp.concatenate(halfway, axis=1))
         solved = []
         for n in range(0, PANEL, block):
             here, below = slice(n, n + block), slice(n, PANEL)
-            solved.append(dot_split(cut(halfway, slice(None), below), cut(inverse, below, here)))
+            solved.append(dot_stacked(cut(halfway, slice(None), below), cut(inverse, below, here)))
         solved = jnp.concatenate(solved, axis=1)
         right = jnp.concatenate(own + [solved], axis=0)
         high, low = split(right.T)

time: 102 us -> 101 us (level)
  Pallas kernels: 55.5 us -> 54.2 us
    pallas_call x1, Pallas kernels: 28.9 us -> 27.5 us  [make_inverse(): pl.pallas_call(chol_kernel, out_shape=jax.ShapeDtypeStruct((PANEL, PANEL)...]
  transfers between devices with their start and end apart: 7 -> 7, of which waited for: 2 -> 2; matrix products, arithmetic and copies ran while one was open for 0% -> 0% of each run, Pallas kernels for 28% -> 27%
where the time goes in v7:
time: 101 us
  Pallas kernels  54.2 us (54%)
  blocking collectives  21.3 us (21%)
  starting transfers between devices  13.5 us (13%)
  waiting for transfers between devices  10.1 us (10%)
  other arithmetic  1.05 us (1%)
    pallas_call x1, Pallas kernels, make_inverse(): pl.pallas_call(chol_kernel, out_shape=jax.ShapeDtypeStruct((PANEL, PANEL)...  27.5 us
    pallas_call x1, Pallas kernels, make_outputs(): pl.pallas_call(functools.partial(panel_kernel, share, row_count, col_coun...  19.2 us
    all_gather x1, blocking collectives, per_device(): columns = lax.all_gather(lead[:TILE], 'row', axis=0, tiled=True)  11.1 us
    all_to_all x1, blocking collectives, per_device(): lax.all_to_all(bucket, 'row', split_axis=0, concat_axis=0, tiled=True)  10.2 us
    ppermute x2, waiting for transfers between devices, exchange(): return lax.ppermute(value, axis, [(i, i ^ step) for i in range(size)])  10.1 us
    pallas_call x1, Pallas kernels, make_features(): pl.pallas_call(functools.partial(feature_kernel, share, row_count), out_s...  5.53 us
    ppermute x3, starting transfers between devices, shift(): lax.ppermute(value, axis, [(i, (i + distance) % size) for i in range(size)])  5.52 us
    ppermute x2, starting transfers between devices, next_tiles(): pieces.append(lax.ppermute(tile, ('row', 'col'), pairs))  5.42 us
  transfers between devices with their start and end apart: 7, of which 2 were waited for; matrix products, arithmetic and copies ran while one was open for 0% of the time, Pallas kernels for 27%

profile of v7, /device:TPU:11, one launch (start us, length us, event | category | flops | bytes accessed | tf_op | source)
XLA Modules:
  0.0 100.9 jit_solution(10970882112226620065)
XLA Ops:
  0.6 5.5 %features.1 = bf16[8,72,256]{2,1,0:T(8,128)(2,1)S(1)} custom-call(s32[1,512]{1,0:T(1,128)} %bitcast.10, bf16[512,768]{1,0:T(8,128)(2,1)} %img_ref.1, bf16[768,2048]{1,0:T(8,128)(2,1)} %win_ref.1, f32[1,2048]{1,0:T(1,128)} %bitcast.9, bf16[2048,256]{1,0:T(8,128)(2,1)} %wout_ref.1, f32[1,256]{1,0:T(1,128)} %bitcast.11), custom_call_target="tpu_custom_call" | custom-call | tf_op jit(solution)/shard_map/features/pallas_call | solution.py:126
  6.2 10.2 %all_to_all.5.recv_ref.refs_0_ = bf16[8,72,256]{2,1,0:T(8,128)(2,1)} all-to-all(bf16[8,72,256]{2,1,0:T(8,128)(2,1)S(1)} %features.1), channel_id=1, replica_groups=mesh['row'=8,'col'=4] {'row'}, dimensions={0} | all-to-all | bytes 589824 | tf_op jit(solution)/shard_map/all_to_all | solution.py:456
  16.4 1.9 %lead.1 = bf16[256,256]{1,0:T(8,128)(2,1)} custom-call(bf16[8,72,256]{2,1,0:T(8,128)(2,1)} %all_to_all.5.recv_ref.refs_0_), custom_call_target="tpu_custom_call" | custom-call | tf_op jit(solution)/shard_map/lead/pallas_call | solution.py:172
  18.2 0.2 collective-permute-start
  18.4 4.6 %collective-permute-done = bf16[256,256]{1,0:T(8,128)(2,1)S(1)} collective-permute-done((bf16[256,256]{1,0:T(8,128)(2,1)}, bf16[256,256]{1,0:T(8,128)(2,1)S(1)}, u32[]{:S(2)}, u32[]{:S(2)}) %collective-permute-start) | collective-permute-done | bytes 131104 | tf_op jit(solution)/shard_map/ppermute | solution.py:420
  23.0 0.9 add.28
  24.0 2.4 %collective-permute-start.1 = (bf16[256,256]{1,0:T(8,128)(2,1)S(1)}, bf16[256,256]{1,0:T(8,128)(2,1)S(1)}, u32[]{:S(2)}, u32[]{:S(2)}) collective-permute-start(bf16[256,256]{1,0:T(8,128)(2,1)S(1)} %add.28), channel_id=1, source_target_pairs={{0,2},{1,3},{2,0},{3,1},{4,6},{5,7},{6,4},{7,5},{8,10},{9,11},{10,... | collective-permute-start | bytes 393224 | tf_op jit(solution)/shard_map/ppermute | solution.py:420
  26.3 0.1 pad_add_fusion.place_ref
  26.4 5.5 %collective-permute-done.1 = bf16[256,256]{1,0:T(8,128)(2,1)S(1)} collective-permute-done((bf16[256,256]{1,0:T(8,128)(2,1)S(1)}, bf16[256,256]{1,0:T(8,128)(2,1)S(1)}, u32[]{:S(2)}, u32[]{:S(2)}) %collective-permute-start.1) | collective-permute-done | bytes 131104 | tf_op jit(solution)/shard_map/ppermute | solution.py:420
  31.9 0.4 collective-permute-start.4
  32.3 2.8 %collective-permute-start.3 = (bf16[8,72,256]{2,1,0:T(8,128)(2,1)}, bf16[8,72,256]{2,1,0:T(8,128)(2,1)S(1)}, u32[]{:S(2)}, u32[]{:S(2)}) collective-permute-start(bf16[8,72,256]{2,1,0:T(8,128)(2,1)} %all_to_all.5.recv_ref.refs_0_), channel_id=1, source_target_pairs={{0,2},{1,3},{2,0},{3,1},{4,6},{5,7},{6,4},{7,5},{8,10},{9,11},{10,... | collective-permute-start | bytes 884744 | tf_op jit(solution)/shard_map/ppermute | solution.py:416
  35.2 2.3 %collective-permute-start.2 = (bf16[8,72,256]{2,1,0:T(8,128)(2,1)}, bf16[8,72,256]{2,1,0:T(8,128)(2,1)S(1)}, u32[]{:S(2)}, u32[]{:S(2)}) collective-permute-start(bf16[8,72,256]{2,1,0:T(8,128)(2,1)} %all_to_all.5.recv_ref.refs_0_), channel_id=1, source_target_pairs={{0,1},{1,2},{2,3},{3,0},{4,5},{5,6},{6,7},{7,4},{8,9},{9,10},{10,1... | collective-permute-start | bytes 884744 | tf_op jit(solution)/shard_map/ppermute | solution.py:416
  37.5 11.1 %all_gather.3.cols_ref.refs_6_ = bf16[1024,256]{1,0:T(8,128)(2,1)S(1)} all-gather(bf16[128,256]{1,0:T(8,128)(2,1)S(1)} %slice.6), channel_id=1, replica_groups=mesh['row'=8,'col'=4] {'row'}, dimensions={0}, use_global_device_ids=true | all-gather | bytes 589824 | tf_op jit(solution)/shard_map/all_gather | solution.py:461
  48.6 0.0 copy-start
  48.6 1.6 %collective-permute-start.6 = (bf16[128,256]{1,0:T(8,128)(2,1)S(1)}, bf16[128,256]{1,0:T(8,128)(2,1)S(1)}, u32[]{:S(2)}, u32[]{:S(2)}) collective-permute-start(bf16[128,256]{1,0:T(8,128)(2,1)S(1)} %slice.7), channel_id=1, source_target_pairs={{16,0},{20,1},{24,2},{28,3},{17,4},{21,5},{25,6},{29,7},{18,8},{22... | collective-permute-start | bytes 196616 | tf_op jit(solution)/shard_map/ppermute | solution.py:441
  50.2 3.8 %collective-permute-start.5 = (bf16[128,256]{1,0:T(8,128)(2,1)S(1)}, bf16[128,256]{1,0:T(8,128)(2,1)S(1)}, u32[]{:S(2)}, u32[]{:S(2)}) collective-permute-start(bf16[128,256]{1,0:T(8,128)(2,1)S(1)} %slice.7), channel_id=1, source_target_pairs={{0,0},{4,1},{8,2},{12,3},{1,4},{5,5},{9,6},{13,7},{2,8},{6,9},{10,... | collective-permute-start | bytes 196616 | tf_op jit(solution)/shard_map/ppermute | solution.py:441
  54.0 27.5 %cholesky.1.refs_7_ = f32[1024,1024]{1,0:T(8,128)S(1)} custom-call(bf16[1024,256]{1,0:T(8,128)(2,1)S(1)} %all_gather.3.cols_ref.refs_6_), custom_call_target="tpu_custom_call" | custom-call | flops 40000000000 | bytes 5242880 | tf_op jit(solution)/shard_map/cholesky/pallas_call | solution.py:278
  81.6 0.0 collective-permute-done.6.refs_5_
  81.6 0.0 collective-permute-done.5.refs_4_
  81.6 0.0 collective-permute-done.4.refs_3_
  81.6 0.0 collective-permute-done.3.refs_2_
  81.6 0.0 collective-permute-done.2.refs_1_
  81.6 0.0 copy-done
  81.6 19.2 %panels.1 = (f32[4096,128]{1,0:T(8,128)}, f32[4096,128]{1,0:T(8,128)}) custom-call(s32[4]{0:T(128)S(1)} %pad_add_fusion.place_ref, bf16[8,72,256]{2,1,0:T(8,128)(2,1)S(1)} %copy-done, bf16[8,72,256]{2,1,0:T(8,128)(2,1)S(1)} %collective-permute-done.2.refs_1_, bf16[8,72,256]{2,1,0:T(8,128)(2,1)S(1)} %collective-permute-done.3.refs_2_, ...), custom_call_target="tpu_custom_call" | custom-call | tf_op jit(solution)/shard_map/panels/pallas_call | solution.py:393
  (3 shorter events, 0.0 us)
Async XLA Ops:
  18.2 4.8 %collective-permute-start = (bf16[256,256]{1,0:T(8,128)(2,1)}, bf16[256,256]{1,0:T(8,128)(2,1)S(1)}, u32[]{:S(2)}, u32[]{:S(2)}) collective-permute-start(bf16[256,256]{1,0:T(8,128)(2,1)} %lead.1), channel_id=1, source_target_pairs={{0,1},{1,0},{2,3},{3,2},{4,5},{5,4},{6,7},{7,6},{8,9},{9,8},{10,11... | collective-permute-start | bytes 393224 | tf_op jit(solution)/shard_map/ppermute | solution.py:420
  24.0 7.9 %collective-permute-start.1 = (bf16[256,256]{1,0:T(8,128)(2,1)S(1)}, bf16[256,256]{1,0:T(8,128)(2,1)S(1)}, u32[]{:S(2)}, u32[]{:S(2)}) collective-permute-start(bf16[256,256]{1,0:T(8,128)(2,1)S(1)} %add.28), channel_id=1, source_target_pairs={{0,2},{1,3},{2,0},{3,1},{4,6},{5,7},{6,4},{7,5},{8,10},{9,11},{10,... | collective-permute-start | bytes 393224 | tf_op jit(solution)/shard_map/ppermute | solution.py:420
  31.9 49.7 %collective-permute-start.4 = (bf16[8,72,256]{2,1,0:T(8,128)(2,1)}, bf16[8,72,256]{2,1,0:T(8,128)(2,1)S(1)}, u32[]{:S(2)}, u32[]{:S(2)}) collective-permute-start(bf16[8,72,256]{2,1,0:T(8,128)(2,1)} %all_to_all.5.recv_ref.refs_0_), channel_id=1, source_target_pairs={{0,3},{1,0},{2,1},{3,2},{4,7},{5,4},{6,5},{7,6},{8,11},{9,8},{10,9... | collective-permute-start | bytes 884744 | tf_op jit(solution)/shard_map/ppermute | solution.py:416
  32.3 49.3 %collective-permute-start.3 = (bf16[8,72,256]{2,1,0:T(8,128)(2,1)}, bf16[8,72,256]{2,1,0:T(8,128)(2,1)S(1)}, u32[]{:S(2)}, u32[]{:S(2)}) collective-permute-start(bf16[8,72,256]{2,1,0:T(8,128)(2,1)} %all_to_all.5.recv_ref.refs_0_), channel_id=1, source_target_pairs={{0,2},{1,3},{2,0},{3,1},{4,6},{5,7},{6,4},{7,5},{8,10},{9,11},{10,... | collective-permute-start | bytes 884744 | tf_op jit(solution)/shard_map/ppermute | solution.py:416
  35.2 46.5 %collective-permute-start.2 = (bf16[8,72,256]{2,1,0:T(8,128)(2,1)}, bf16[8,72,256]{2,1,0:T(8,128)(2,1)S(1)}, u32[]{:S(2)}, u32[]{:S(2)}) collective-permute-start(bf16[8,72,256]{2,1,0:T(8,128)(2,1)} %all_to_all.5.recv_ref.refs_0_), channel_id=1, source_target_pairs={{0,1},{1,2},{2,3},{3,0},{4,5},{5,6},{6,7},{7,4},{8,9},{9,10},{10,1... | collective-permute-start | bytes 884744 | tf_op jit(solution)/shard_map/ppermute | solution.py:416
  48.6 33.0 %copy-start = (bf16[8,72,256]{2,1,0:T(8,128)(2,1)S(1)}, bf16[8,72,256]{2,1,0:T(8,128)(2,1)}, u32[]{:S(2)}) copy-start(bf16[8,72,256]{2,1,0:T(8,128)(2,1)} %all_to_all.5.recv_ref.refs_0_) | copy-start | bytes 884740
  48.6 33.0 %collective-permute-start.6 = (bf16[128,256]{1,0:T(8,128)(2,1)S(1)}, bf16[128,256]{1,0:T(8,128)(2,1)S(1)}, u32[]{:S(2)}, u32[]{:S(2)}) collective-permute-start(bf16[128,256]{1,0:T(8,128)(2,1)S(1)} %slice.7), channel_id=1, source_target_pairs={{16,0},{20,1},{24,2},{28,3},{17,4},{21,5},{25,6},{29,7},{18,8},{22... | collective-permute-start | bytes 196616 | tf_op jit(solution)/shard_map/ppermute | solution.py:441
  50.2 31.4 %collective-permute-start.5 = (bf16[128,256]{1,0:T(8,128)(2,1)S(1)}, bf16[128,256]{1,0:T(8,128)(2,1)S(1)}, u32[]{:S(2)}, u32[]{:S(2)}) collective-permute-start(bf16[128,256]{1,0:T(8,128)(2,1)S(1)} %slice.7), channel_id=1, source_target_pairs={{0,0},{4,1},{8,2},{12,3},{1,4},{5,5},{9,6},{13,7},{2,8},{6,9},{10,... | collective-permute-start | bytes 196616 | tf_op jit(solution)/shard_map/ppermute | solution.py:441
